TPU v7x, 32 devices: a whole 2x2x4 slice. The times are simulated.
32 devices in a mesh: order: 4 (over y, x), chan: 8 (over z, core).
Axes of the slice: x: 2, y: 2, z: 4, core: 2. Of those that a mesh axis runs over, the one named last changes fastest.
Arguments:
- grad_out: bfloat16 [3, 256, 720, 1440], P(None, 'chan', 'order'), may hold values from -6 to 6
- legendre: bfloat16 [48, 720, 768], P('order', 'chan'), as said below
- filter_re: float32 [256, 720], P('chan'), may hold values from -6 to 6
- filter_im: float32 [256, 720], P('chan'), may hold values from -6 to 6
- quad_weight: float32 [720], P('order'), may hold values from 0.5 to 2
- pair_order: int32 [48], replicated, may hold values from 0 to 359, as said below
Outputs:
- grad_in: bfloat16 [3, 256, 720, 1440], P(None, 'chan', 'order')
Inputs may be any that keep to these rules, and one draw needn't show every extreme that they name: `pair_order`: the values are distinct. Slot j belongs to index j // 12 of order. `legendre`: entries in rows r > 720 of the last dimension are zero.
All inputs are finite; a program needn't handle non-finite values.
Results may differ from a plain program's by a relative error of at most 0.0072.
Values may be sent and summed in bfloat16 or wider, within the bound.
A program may use at most 256 MiB of HBM per device.

v0:
```python
import functools
import math

import jax
import jax.numpy as jnp
from jax import lax
from jax.experimental import pallas as pl
from jax.experimental.pallas import tpu as pltpu
from jax.sharding import PartitionSpec as P

NLON = 1440
M = 720


def step_of(count, most):
    return max(d for d in range(1, most + 1) if count % d == 0)


def basis_tables(pair_order, devices, rows):
    low = pair_order.reshape(devices, -1)
    per = low.shape[1]
    orders = jnp.stack([low, low, M - 1 - low, M - 1 - low], axis=1)
    orders = jnp.pad(orders, ((0, 0), (0, 0), (0, rows - per))).reshape(-1)
    shape = (devices, 4, rows)
    real = (lax.broadcasted_iota(jnp.int32, shape, 1) % 2 == 0).reshape(-1)
    live = (lax.broadcasted_iota(jnp.int32, shape, 2) < per).reshape(-1)
    longitude = jnp.arange(NLON, dtype=jnp.int32)

    def table(phases, real, live):
        angles = (phases % NLON).astype(jnp.float32) * (2.0 * math.pi / NLON)
        values = jnp.where(real, jnp.cos(angles), -jnp.sin(angles))
        return jnp.where(live, values, 0.0)

    inverse = table(orders[:, None] * longitude[None, :], real[:, None], live[:, None])
    factor = jnp.where(orders == 0, 1.0, 2.0).astype(jnp.float32)
    forward = (inverse * factor[:, None]).astype(jnp.bfloat16).T
    return forward, inverse.astype(jnp.bfloat16)


def pair_gains(low_order, filter_re, filter_im, packed_rows):
    both = jnp.concatenate([filter_re, filter_im], axis=0).T
    width = both.shape[1]
    padded = jnp.concatenate([both, jnp.zeros((packed_rows, width), jnp.float32)], axis=0)
    tail = jnp.broadcast_to(both[M - 1 : M], (packed_rows - 1 - M, width))
    shifted = jnp.concatenate([both[:1], both, tail], axis=0)
    row_ids = jnp.arange(packed_rows, dtype=jnp.int32)
    below = row_ids[None, :] < (M - low_order)[:, None]
    gathered = []
    for index in range(low_order.shape[0]):
        upper = lax.dynamic_slice_in_dim(padded, low_order[index], packed_rows, 0)
        gathered.append(jnp.where(below[index][:, None], upper, shifted))
    return jnp.stack(gathered, axis=0)


def forward_kernel(x_ref, table_ref, out_ref, *, devices, rows):
    samples, steps, channels, longitudes = x_ref.shape
    sc = samples * channels
    pieces = [x_ref[s, t] for t in range(steps) for s in range(samples)]
    block = jnp.concatenate(pieces, axis=0)
    coeffs = jnp.dot(block, table_ref[...], preferred_element_type=jnp.float32)
    coeffs = coeffs.astype(jnp.bfloat16)
    for t in range(steps):
        turned = coeffs[t * sc : (t + 1) * sc].T
        for d in range(devices):
            parts = [turned[(4 * d + q) * rows : (4 * d + q + 1) * rows] for q in range(4)]
            out_ref[d, t] = jnp.concatenate(parts, axis=1)


def inverse_kernel(scale_ref, band_ref, table_ref, out_ref):
    devices, steps, rows, lanes = band_ref.shape
    samples, _, channels, longitudes = out_ref.shape
    sc = lanes // 4
    turned = []
    for t in range(steps):
        parts = []
        for d in range(devices):
            block = band_ref[d, t]
            parts += [block[:, q * sc : (q + 1) * sc] for q in range(4)]
        turned.append(jnp.concatenate(parts, axis=0).T)
    block = jnp.concatenate(turned, axis=0)
    values = jnp.dot(block, table_ref[...], preferred_element_type=jnp.float32)
    start = pl.program_id(0) * steps
    for t in range(steps):
        scale = scale_ref[start + t]
        for s in range(samples):
            row = t * sc + s * channels
            out_ref[s, t] = (values[row : row + channels] * scale).astype(jnp.bfloat16)


def middle_kernel(low_ref, legendre_ref, coeffs_ref, gains_ref, out_ref, *, samples):
    legendre = legendre_ref[0]
    packed_rows = legendre.shape[1]
    half = coeffs_ref.shape[2] // 2
    sc = half // 2
    channels = sc // samples
    contract = (((0,), (0,)), ((), ()))
    spectrum = lax.dot_general(legendre, coeffs_ref[0], contract, preferred_element_type=jnp.float32)
    row_ids = lax.broadcasted_iota(jnp.int32, (packed_rows, half), 0)
    inside = row_ids < M - low_ref[pl.program_id(0)]
    own = jnp.where(inside, spectrum[:, :half], spectrum[:, half:])
    other = jnp.concatenate([own[:, sc:], own[:, :sc]], axis=1)
    gains = gains_ref[0]
    gain_re = gains[:, :channels]
    gain_im = gains[:, channels:]
    gain_re = jnp.concatenate([gain_re] * (2 * samples), axis=1)
    gain_im = jnp.concatenate([gain_im] * samples + [-gain_im] * samples, axis=1)
    filtered = gain_re * own + gain_im * other
    zeros = jnp.zeros_like(filtered)
    split = jnp.concatenate([jnp.where(inside, filtered, zeros), jnp.where(inside, zeros, filtered)], axis=1)
    synthesis = jnp.dot(legendre, split.astype(jnp.bfloat16), preferred_element_type=jnp.float32)
    out_ref[0] = synthesis.astype(jnp.bfloat16)


def body(grad_out, legendre, filter_re, filter_im, quad_weight, pair_order, *, devices):
    samples, channels, lat_local, longitudes = grad_out.shape
    pairs_dev, _, packed_rows = legendre.shape
    rows = -(-pairs_dev // 16) * 16
    lanes = 4 * samples * channels
    columns = devices * 4 * rows
    steps = step_of(lat_local, 10)
    whole = lax.all_gather(legendre, "chan", axis=1, tiled=True)
    forward, inverse = basis_tables(pair_order, devices, rows)
    grid_block = pl.BlockSpec((samples, steps, channels, longitudes), lambda i: (0, i, 0, 0))
    band_block = pl.BlockSpec((devices, steps, rows, lanes), lambda i: (0, i, 0, 0))
    params = pltpu.CompilerParams(dimension_semantics=("arbitrary",), vmem_limit_bytes=56 << 20)
    coeffs = pl.pallas_call(
        functools.partial(forward_kernel, devices=devices, rows=rows),
        grid=(lat_local // steps,),
        in_specs=[grid_block, pl.BlockSpec((longitudes, columns), lambda i: (0, 0))],
        out_specs=band_block,
        out_shape=jax.ShapeDtypeStruct((devices, lat_local, rows, lanes), jnp.bfloat16),
        compiler_params=params,
        name="fourier",
    )(jnp.transpose(grad_out, (0, 2, 1, 3)), forward)
    gathered = lax.all_to_all(coeffs, "order", split_axis=0, concat_axis=0, tiled=True)
    latitudes = devices * lat_local
    gathered = gathered.reshape(latitudes, rows, lanes)[:, :pairs_dev]
    gathered = jnp.transpose(gathered, (1, 0, 2))
    start_slot = lax.axis_index("order") * pairs_dev
    low_order = lax.dynamic_slice_in_dim(pair_order, start_slot, pairs_dev)
    gains = pair_gains(low_order, filter_re, filter_im, packed_rows)
    synthesis = pl.pallas_call(
        functools.partial(middle_kernel, samples=samples),
        grid=(pairs_dev,),
        in_specs=[
            pl.BlockSpec(memory_space=pltpu.SMEM),
            pl.BlockSpec((1, latitudes, packed_rows), lambda i: (i, 0, 0)),
            pl.BlockSpec((1, latitudes, lanes), lambda i: (i, 0, 0)),
            pl.BlockSpec((1, packed_rows, 2 * channels), lambda i: (i, 0, 0)),
        ],
        out_specs=pl.BlockSpec((1, latitudes, lanes), lambda i: (i, 0, 0)),
        out_shape=jax.ShapeDtypeStruct((pairs_dev, latitudes, lanes), jnp.bfloat16),
        compiler_params=params,
        name="legendre",
    )(low_order, whole, gathered, gains)
    synthesis = jnp.transpose(synthesis, (1, 0, 2))
    synthesis = jnp.pad(synthesis, ((0, 0), (0, rows - pairs_dev), (0, 0)))
    synthesis = synthesis.reshape(devices, lat_local, rows, lanes)
    band = lax.all_to_all(synthesis, "order", split_axis=0, concat_axis=0, tiled=True)
    scale = quad_weight * (2.0 * math.pi / NLON)
    values = pl.pallas_call(
        inverse_kernel,
        grid=(lat_local // steps,),
        in_specs=[
            pl.BlockSpec(memory_space=pltpu.SMEM),
            band_block,
            pl.BlockSpec((columns, longitudes), lambda i: (0, 0)),
        ],
        out_specs=grid_block,
        out_shape=jax.ShapeDtypeStruct((samples, lat_local, channels, longitudes), jnp.bfloat16),
        compiler_params=params,
        name="fourier_back",
    )(scale, band, inverse)
    return jnp.transpose(values, (0, 2, 1, 3))


def solution(mesh):
    in_specs = (
        P(None, "chan", "order", None),
        P("order", "chan", None),
        P("chan", None),
        P("chan", None),
        P("order"),
        P(),
    )
    out_specs = P(None, "chan", "order", None)
    local = functools.partial(body, devices=mesh.shape["order"])
    return jax.shard_map(local, mesh=mesh, in_specs=in_specs, out_specs=out_specs, check_vma=False)
```

profile of v0, /device:TPU:0, one launch (start us, length us, event | category | flops | bytes accessed | tf_op | source)
XLA Modules:
  0.0 372.1 jit_solution(7717177332331776054)
XLA Ops:
  6.5 3.8 %copy.16 = bf16[12,90,768]{2,0,1:T(8,128)(2,1)} copy(bf16[12,90,768]{2,1,0:T(8,128)(2,1)} %param.7) | data formatting | bytes 3317760 | tf_op args[1]
  10.8 7.2 %multiply_convert_fusion.table_ref = bf16[1440,256]{1,0:T(8,128)(2,1)} fusion(f32[256]{0:T(256)S(1)} %compare_select_fusion, s32[256]{0:T(256)S(1)} %mul.54, pred[256]{0:T(512)(128)(4,1)S(1)} %eq.28, pred[256]{0:T(512)(128)(4,1)S(1)} %broadcast_in_dim.137), kind=kLoop, calls=%fused_computation.24 | loop fusion | flops 5160960 | bytes 739840 | tf_op jit(solution)/shard_map/convert_element_type | solution.py:36
  18.1 33.6 %fourier.1 = bf16[4,180,16,384]{3,2,1,0:T(8,128)(2,1)} custom-call(bf16[3,180,32,1440]{3,2,1,0:T(8,128)(2,1)} %bitcast.73, bf16[1440,256]{1,0:T(8,128)(2,1)} %multiply_convert_fusion.table_ref), custom_call_target="tpu_custom_call" | custom-call | tf_op jit(solution)/shard_map/fourier/pallas_call | solution.py:126
  51.7 6.1 %all-to-all-start = ((bf16[4,180,16,384]{3,2,1,0:T(8,128)(2,1)}), bf16[4,180,16,384]{3,2,1,0:T(8,128)(2,1)}, u32[]{:S(2)}, u32[]{:S(2)}) async-start(bf16[4,180,16,384]{3,2,1,0:T(8,128)(2,1)} %fourier.1), calls=%async_computation | async-start | bytes 17694720 | tf_op jit(solution)/shard_map/all_to_all | solution.py:135
  57.9 0.7 fusion.47
  73.6 0.2 copy.19
  73.8 0.2 copy.20
  81.6 0.2 maximum_bitcast_fusion
  81.8 0.9 fusion.12
  82.7 0.9 fusion.15
  83.7 0.9 fusion.18
  84.6 1.0 fusion.21
  85.5 0.9 fusion.24
  86.5 0.9 fusion.27
  87.4 0.9 fusion.30
  88.3 0.9 fusion.33
  89.3 0.9 fusion.36
  90.2 0.9 fusion.39
  91.1 0.9 fusion.42
  92.1 0.9 fusion.45.gains_ref
  93.0 63.8 %all-to-all-done = bf16[4,180,16,384]{3,2,1,0:T(8,128)(2,1)} async-done(((bf16[4,180,16,384]{3,2,1,0:T(8,128)(2,1)}), bf16[4,180,16,384]{3,2,1,0:T(8,128)(2,1)}, u32[]{:S(2)}, u32[]{:S(2)}) %all-to-all-start) | async-done | bytes 8847392 | tf_op jit(solution)/shard_map/all_to_all | solution.py:135
  156.8 7.8 %copy.27 = bf16[720,12,384]{2,0,1:T(8,128)(2,1)} copy(bf16[720,12,384]{2,1,0:T(8,128)(2,1)} %bitcast.72) | data formatting | bytes 13271040
  164.6 7.2 %all-gather.2.cloned.1.call-done = bf16[12,720,768]{2,0,1:T(8,128)(2,1)} async-done(((bf16[12,90,768]{2,0,1:T(8,128)(2,1)}), bf16[12,720,768]{2,0,1:T(8,128)(2,1)}) %all-gather.2.cloned.1.call-update) | async-done | bytes 13271056 | tf_op jit(solution)/shard_map/all_gather | solution.py:121
  171.8 14.7 %copy.21.legendre_ref = bf16[12,720,768]{2,1,0:T(8,128)(2,1)} copy(bf16[12,720,768]{2,0,1:T(8,128)(2,1)} %all-gather.2.cloned.1.call-done) | data formatting | bytes 26542080 | tf_op jit(solution)/shard_map/all_gather | solution.py:121
  186.6 29.4 %legendre.1 = bf16[12,720,384]{2,1,0:T(8,128)(2,1)} custom-call(s32[12]{0:T(128)} %copy-done, bf16[12,720,768]{2,1,0:T(8,128)(2,1)} %copy.21.legendre_ref, bf16[12,720,384]{2,1,0:T(8,128)(2,1)} %bitcast.75, f32[12,768,64]{2,1,0:T(8,128)} %fusion.45.gains_ref), custom_call_target="tpu_custom_call" | custom-call | tf_op jit(solution)/shard_map/legendre/pallas_call | solution.py:142
  215.9 8.1 %copy.25 = bf16[720,12,384]{2,1,0:T(8,128)(2,1)} copy(bf16[720,12,384]{2,0,1:T(8,128)(2,1)} %bitcast.76) | data formatting | bytes 13271040
  224.1 8.1 %pad.10.clone = bf16[720,16,384]{2,1,0:T(8,128)(2,1)} pad(bf16[720,12,384]{2,1,0:T(8,128)(2,1)} %copy.25, bf16[]{:T(256)} %constant.57.clone.1), padding=0_0x0_4x0_0 | pad | bytes 15482882 | tf_op jit(solution)/shard_map/jit(_pad)/pad | solution.py:157
  232.2 5.9 %all-to-all-start.1 = ((bf16[4,180,16,384]{3,2,1,0:T(8,128)(2,1)}), bf16[4,180,16,384]{3,2,1,0:T(8,128)(2,1)}, u32[]{:S(2)}, u32[]{:S(2)}) async-start(bf16[4,180,16,384]{3,2,1,0:T(8,128)(2,1)} %bitcast.74), calls=%async_computation.1 | async-start | bytes 17694720 | tf_op jit(solution)/shard_map/all_to_all | solution.py:159
  238.1 0.6 broadcast_multiply_fusion.scale_ref
  238.6 8.1 %select_convert_fusion.table_ref = bf16[256,1440]{1,0:T(8,128)(2,1)} fusion(s32[256]{0:T(256)S(1)} %mul.54, pred[256]{0:T(512)(128)(4,1)S(1)} %eq.28, pred[256]{0:T(512)(128)(4,1)S(1)} %broadcast_in_dim.137), kind=kLoop, calls=%fused_computation.17 | loop fusion | flops 4792320 | bytes 738816 | tf_op jit(solution)/shard_map/convert_element_type | solution.py:37
  246.7 89.4 %all-to-all-done.1.band_ref = bf16[4,180,16,384]{3,2,1,0:T(8,128)(2,1)} async-done(((bf16[4,180,16,384]{3,2,1,0:T(8,128)(2,1)}), bf16[4,180,16,384]{3,2,1,0:T(8,128)(2,1)}, u32[]{:S(2)}, u32[]{:S(2)}) %all-to-all-start.1) | async-done | bytes 8847392 | tf_op jit(solution)/shard_map/all_to_all | solution.py:159
  336.1 29.2 %fourier_back.1 = bf16[3,180,32,1440]{3,2,1,0:T(8,128)(2,1)} custom-call(f32[180]{0:T(256)} %broadcast_multiply_fusion.scale_ref, bf16[4,180,16,384]{3,2,1,0:T(8,128)(2,1)} %all-to-all-done.1.band_ref, bf16[256,1440]{1,0:T(8,128)(2,1)} %select_convert_fusion.table_ref), custom_call_target="tpu_custom_call" | custom-call | tf_op jit(solution)/shard_map/fourier_back/pallas_call | solution.py:161
  (31 shorter events, 0.8 us)
Async XLA Ops:
  6.5 4.1 %copy-start.3 = (s32[48]{0:T(128)S(1)}, s32[48]{0:T(128)}, u32[]{:S(2)}) copy-start(s32[48]{0:T(128)} %param.11) | copy-start | bytes 580
  6.5 165.3 %all-gather.2.cloned.1.call-start = ((), (), s32[]{:S(2)}) async-start(), calls=%async_computation.2 | async-start | bytes 19906560 | tf_op jit(solution)/shard_map/all_gather | solution.py:121
  51.7 21.9 %copy-start.1 = (f32[32,720]{1,0:T(8,128)S(1)}, f32[32,720]{1,0:T(8,128)}, u32[]{:S(2)}) copy-start(f32[32,720]{1,0:T(8,128)} %param.8) | copy-start | bytes 276484
  51.7 22.0 %copy-start.2 = (f32[32,720]{1,0:T(8,128)S(1)}, f32[32,720]{1,0:T(8,128)}, u32[]{:S(2)}) copy-start(f32[32,720]{1,0:T(8,128)} %param.9) | copy-start | bytes 276484
  51.7 105.1 %all-to-all-start = ((bf16[4,180,16,384]{3,2,1,0:T(8,128)(2,1)}), bf16[4,180,16,384]{3,2,1,0:T(8,128)(2,1)}, u32[]{:S(2)}, u32[]{:S(2)}) async-start(bf16[4,180,16,384]{3,2,1,0:T(8,128)(2,1)} %fourier.1), calls=%async_computation | async-start | bytes 17694720 | tf_op jit(solution)/shard_map/all_to_all | solution.py:135
  57.9 33.3 %copy-start = (s32[12]{0:T(128)}, s32[12]{0:T(128)S(1)}, u32[]{:S(2)}) copy-start(s32[12]{0:T(128)S(1)} %get-tuple-element.18.low_ref) | copy-start | bytes 148
  232.2 5.9 %copy-start.4 = (f32[180]{0:T(256)S(1)}, f32[180]{0:T(256)}, u32[]{:S(2)}) copy-start(f32[180]{0:T(256)} %param.10) | copy-start | bytes 2164
  232.2 103.9 %all-to-all-start.1 = ((bf16[4,180,16,384]{3,2,1,0:T(8,128)(2,1)}), bf16[4,180,16,384]{3,2,1,0:T(8,128)(2,1)}, u32[]{:S(2)}, u32[]{:S(2)}) async-start(bf16[4,180,16,384]{3,2,1,0:T(8,128)(2,1)} %bitcast.74), calls=%async_computation.1 | async-start | bytes 17694720 | tf_op jit(solution)/shard_map/all_to_all | solution.py:159
Sparse Core Ops, SparseCore 0:
  10.5 161.3 all-gather.1
where the time goes:
time: 374 us; the launch traced here: 372 us
  waiting for transfers between devices  160 us (43%)
  Pallas kernels  92.2 us (25%)
  local copies, waits for them, and re-layouts  44.1 us (12%)
  between operations  36 us (10%)
  other arithmetic  27.5 us (7%)
  starting transfers between devices  11.9 us (3%)
    all_to_all x1, waiting for transfers between devices, body(): lax.all_to_all(synthesis, 'order', split_axis=0, concat_axis=0, tiled=True)  89.4 us
    all_to_all x1, waiting for transfers between devices, body(): lax.all_to_all(coeffs, 'order', split_axis=0, concat_axis=0, tiled=True)  63.8 us
    pallas_call x1, Pallas kernels, body(): pl.pallas_call(functools.partial(forward_kernel, devices=devices, rows=ro...  33.6 us
    pallas_call x1, Pallas kernels, body(): pl.pallas_call(functools.partial(middle_kernel, samples=samples), grid=(p...  29.4 us
    pallas_call x1, Pallas kernels, body(): pl.pallas_call(inverse_kernel, grid=(lat_local // steps,), in_specs=[pl.B...  29.2 us
    unnamed x16, local copies, waits for them, and re-layouts  20.1 us
    all_gather x1, local copies, waits for them, and re-layouts, body(): whole = lax.all_gather(legendre, 'chan', axis=1, tiled=True)  14.7 us
    unnamed x11, other arithmetic  10.3 us
  transfers between devices with their start and end apart: 3, of which 3 were waited for; matrix products, arithmetic and copies ran while one was open for 10% of the time, Pallas kernels for 9%

commit v1 on v0

v1 whole, which is shorter than its diff:
```python
import functools
import math

import jax
import jax.numpy as jnp
from jax import lax
from jax.experimental import pallas as pl
from jax.experimental.pallas import tpu as pltpu
from jax.sharding import PartitionSpec as P

NLON = 1440
M = 720
TILE = 16
MESH = pl.DeviceIdType.MESH


def step_of(count, most):
    return max(d for d in range(1, most + 1) if count % d == 0)


def basis_tables(pair_order):
    low = pair_order
    orders = jnp.stack([low, low, M - 1 - low, M - 1 - low], axis=1).reshape(-1)
    columns = orders.shape[0]
    real = jnp.arange(columns, dtype=jnp.int32) % 2 == 0
    longitude = jnp.arange(NLON, dtype=jnp.int32)

    def table(phases, real):
        angles = (phases % NLON).astype(jnp.float32) * (2.0 * math.pi / NLON)
        return jnp.where(real, jnp.cos(angles), -jnp.sin(angles))

    inverse = table(orders[:, None] * longitude[None, :], real[:, None])
    factor = jnp.where(orders == 0, 1.0, 2.0).astype(jnp.float32)
    forward = (inverse * factor[:, None]).astype(jnp.bfloat16)
    wide = -(-columns // 128) * 128
    forward = jnp.pad(forward, ((0, wide - columns), (0, 0))).T
    inverse = inverse.astype(jnp.bfloat16).reshape(-1, 4, NLON)
    return forward, jnp.transpose(inverse, (1, 0, 2)).reshape(columns, NLON)


class Line:
    def __init__(self, chips, first, pairs, groups, source, table, sems):
        self.chips, self.first, self.pairs, self.groups = chips, first, pairs, groups
        self.source, self.table = source, table
        self.up_recv, self.down_recv, self.flags = sems
        self.index = lax.axis_index("chan")
        self.place = self.index // 2
        self.partner = self.index + 1 - 2 * (self.index % 2)
        self.share = pairs // groups

    def remote(self, src, dst, send, recv, target):
        return pltpu.make_async_remote_copy(
            src_ref=src, dst_ref=dst, send_sem=send, recv_sem=recv, device_id={"chan": target}, device_id_type=MESH
        )

    def own(self):
        src = self.source.at[pl.ds(self.first, self.pairs)]
        return pltpu.make_async_copy(src, self.table.at[:, self.index], self.flags.at[0])

    def start(self):
        self.own().start()
        src = self.source.at[pl.ds(self.first, self.pairs)]
        self.remote(src, self.table.at[:, self.index], self.flags.at[1], self.flags.at[2], self.partner).start()
        for group in range(self.groups):
            src = self.source.at[pl.ds(self.first + group * self.share, self.share)]
            dst = self.table.at[pl.ds(group * self.share, self.share), self.index]

            @pl.when(self.place < self.chips - 1)
            def _():
                self.remote(src, dst, self.flags.at[3], self.up_recv.at[0, group], self.index + 2).start()

            @pl.when(self.place > 0)
            def _():
                self.remote(src, dst, self.flags.at[4], self.down_recv.at[0, group], self.index - 2).start()

    def step(self, hop, group):
        rows = pl.ds(group * self.share, self.share)

        @pl.when(self.place >= hop)
        def _():
            block = self.table.at[rows, self.index - 2 * hop]
            self.remote(block, block, self.flags.at[3], self.up_recv.at[hop - 1, group], self.index - 2).wait_recv()

            @pl.when(self.place < self.chips - 1)
            def _():
                self.remote(block, block, self.flags.at[3], self.up_recv.at[hop, group], self.index + 2).start()

            self.remote(block, block, self.flags.at[1], self.flags.at[2], self.partner).start()

        @pl.when(self.place + hop < self.chips)
        def _():
            block = self.table.at[rows, self.index + 2 * hop]
            self.remote(block, block, self.flags.at[4], self.down_recv.at[hop - 1, group], self.index + 2).wait_recv()

            @pl.when(self.place > 0)
            def _():
                self.remote(block, block, self.flags.at[4], self.down_recv.at[hop, group], self.index - 2).start()

            self.remote(block, block, self.flags.at[1], self.flags.at[2], self.partner).start()

    def finish(self):
        self.own().wait()
        total = self.table.at[:, pl.ds(0, self.chips)]
        every = self.remote(total, total, self.flags.at[1], self.flags.at[2], self.partner)
        every.wait_send()
        every.wait_recv()
        for place in range(self.chips):
            if place < self.chips - 1:

                @pl.when(self.place == place)
                def _():
                    part = self.table.at[:, pl.ds(0, place + 1)]
                    self.remote(part, part, self.flags.at[3], self.flags.at[2], self.partner).wait_send()

            if place > 0:

                @pl.when(self.place == place)
                def _():
                    part = self.table.at[:, pl.ds(0, self.chips - place)]
                    self.remote(part, part, self.flags.at[4], self.flags.at[2], self.partner).wait_send()


def enter(devices, chips):
    order = lax.axis_index("order")
    index = lax.axis_index("chan")
    place = index // 2
    barrier = pltpu.get_barrier_semaphore()
    for turn in range(1, devices):
        peer = lax.rem(order + turn, devices)
        pl.semaphore_signal(barrier, inc=1, device_id={"order": peer}, device_id_type=MESH)
    partner = index + 1 - 2 * (index % 2)
    pl.semaphore_signal(barrier, inc=1, device_id={"chan": partner}, device_id_type=MESH)

    @pl.when(place < chips - 1)
    def _():
        pl.semaphore_signal(barrier, inc=1, device_id={"chan": index + 2}, device_id_type=MESH)

    @pl.when(place > 0)
    def _():
        pl.semaphore_signal(barrier, inc=1, device_id={"chan": index - 2}, device_id_type=MESH)

    near = jnp.minimum(place, 1) + jnp.minimum(chips - 1 - place, 1)
    pl.semaphore_wait(barrier, devices + near)


def to_order(src, dst, send, recv, peer):
    return pltpu.make_async_remote_copy(
        src_ref=src, dst_ref=dst, send_sem=send, recv_sem=recv, device_id={"order": peer}, device_id_type=MESH
    )


def forward_kernel(
    x_ref, table_ref, legendre_ref, out_ref, gathered_ref, x_buf, turned_ref, stage_ref,
    x_sem, send_sem, recv_sem, own_sem, up_sem, down_sem, flag_sem, *, devices, chips, groups, block_rows
):
    samples, lat_local, channels, _ = x_ref.shape
    pairs, blocks, padded, lanes = out_ref.shape
    sc = samples * channels
    order = lax.axis_index("order")
    per_band = blocks // devices
    per_block = padded // TILE
    chunks = per_band * per_block
    slack = max(0, (per_band - 1) * block_rows + padded - lat_local)
    line = Line(chips, 0, gathered_ref.shape[0], groups, legendre_ref, gathered_ref, (up_sem, down_sem, flag_sem))

    def x_copy(chunk):
        start = (chunk // per_block) * block_rows + (chunk % per_block) * TILE
        back = jnp.maximum(start + TILE - lat_local, 0)
        slot = chunk % 2
        return pltpu.make_async_copy(
            x_ref.at[:, pl.ds(start - back, TILE)], x_buf.at[slot, :, pl.ds(slack - back, TILE)], x_sem.at[slot]
        )

    x_copy(0).start()
    enter(devices, chips)
    line.start()
    steps = (chips - 1) * groups

    def body(chunk, carry):
        slot = chunk % 2
        x_copy(chunk).wait()

        @pl.when(chunk + 1 < chunks)
        def _():
            x_copy(chunk + 1).start()

        pieces = [x_buf[slot, s, slack + t] for t in range(TILE) for s in range(samples)]
        coeffs = jnp.dot(jnp.concatenate(pieces, axis=0), table_ref[...], preferred_element_type=jnp.float32)
        for t in range(TILE):
            turned = coeffs[t * sc : (t + 1) * sc].T
            turned_ref[t, :, 0:sc] = turned[: turned_ref.shape[1]]
        block, part = chunk // per_block, chunk % per_block
        live = lax.broadcasted_iota(jnp.int32, (TILE, lanes), 0) < block_rows - part * TILE
        for pair in range(devices * pairs):
            row = jnp.concatenate([turned_ref[:, 4 * pair + q, 0:sc] for q in range(4)], axis=1)
            stage_ref[chunk, pair] = jnp.where(live, row, 0.0).astype(jnp.bfloat16)
        target = out_ref.at[:, order * per_band + block, pl.ds(part * TILE, TILE)]
        for turn in range(1, devices):
            peer = lax.rem(order + turn, devices)
            src = stage_ref.at[chunk, pl.ds(peer * pairs, pairs)]
            to_order(src, target, send_sem.at[turn], recv_sem.at[turn], peer).start()
        pltpu.make_async_copy(stage_ref.at[chunk, pl.ds(order * pairs, pairs)], target, own_sem).start()
        step = chunk - 1

        @pl.when((step >= 0) & (step < steps))
        def _():
            line.step(step // groups + 1, step % groups)

        return carry

    lax.fori_loop(0, chunks, body, 0)
    if steps > chunks - 1:

        def rest(step, carry):
            line.step(step // groups + 1, step % groups)
            return carry

        lax.fori_loop(chunks - 1, steps, rest, 0)
    for turn in range(1, devices):
        peer = lax.rem(order + turn, devices)
        source = lax.rem(order + devices - turn, devices)
        sent = out_ref.at[:, pl.ds(peer * per_band, per_band)]
        got = out_ref.at[:, pl.ds(source * per_band, per_band)]
        both = to_order(sent, got, send_sem.at[turn], recv_sem.at[turn], peer)
        both.wait_send()
        both.wait_recv()
    own = out_ref.at[:, pl.ds(order * per_band, per_band)]
    pltpu.make_async_copy(own, own, own_sem).wait()
    line.finish()


def middle_kernel(
    low_ref, coeffs_ref, early_ref, legendre_ref, gains_ref, shifted_ref, out_ref, late_ref, z_buf, l_buf, stage_ref,
    z_sem, l_sem, send_sem, recv_sem, own_sem, up_sem, down_sem, flag_sem, *, devices, chips, groups, samples
):
    pairs, blocks, padded, lanes = coeffs_ref.shape
    packed_rows = legendre_ref.shape[2]
    early = early_ref.shape[0]
    rows = blocks * padded
    band = rows // devices
    half = lanes // 2
    sc = half // 2
    channels = sc // samples
    order = lax.axis_index("order")
    line = Line(chips, early, pairs - early, groups, legendre_ref, late_ref, (up_sem, down_sem, flag_sem))

    def z_copy(pair):
        return pltpu.make_async_copy(coeffs_ref.at[pair], z_buf.at[pair % 2], z_sem.at[pair % 2])

    def l_copy(ref, entry, slot):
        return pltpu.make_async_copy(ref.at[entry], l_buf.at[slot], l_sem.at[slot])

    z_copy(0).start()
    l_copy(early_ref, 0, 0).start()
    enter(devices, chips)
    line.start()
    steps = (chips - 1) * groups
    contract = (((0,), (0,)), ((), ()))
    row_ids = lax.broadcasted_iota(jnp.int32, (packed_rows, half), 0)

    def body(pair, carry):
        slot = pair % 2
        z_copy(pair).wait()
        l_copy(early_ref, 0, slot).wait()

        @pl.when(pair + 1 < pairs)
        def _():
            z_copy(pair + 1).start()

        @pl.when(pair + 1 < early)
        def _():
            l_copy(early_ref, pair + 1, 1 - slot).start()

        @pl.when((pair + 1 >= early + 1) & (pair + 1 < pairs))
        def _():
            l_copy(late_ref, pair + 1 - early, 1 - slot).start()

        legendre = l_buf[slot].reshape(rows, packed_rows)
        coeffs = z_buf[slot].reshape(rows, lanes)
        spectrum = lax.dot_general(legendre, coeffs, contract, preferred_element_type=jnp.float32)
        low = low_ref[pair]
        inside = row_ids < M - low
        own = jnp.where(inside, spectrum[:, :half], spectrum[:, half:])
        other = jnp.concatenate([own[:, sc:], own[:, :sc]], axis=1)
        gains = jnp.where(inside[:, : 2 * channels], gains_ref[pl.ds(low, packed_rows), :], shifted_ref[...])
        gain_re = gains[:, :channels]
        gain_im = gains[:, channels:]
        gain_re = jnp.concatenate([gain_re] * (2 * samples), axis=1)
        gain_im = jnp.concatenate([gain_im] * samples + [-gain_im] * samples, axis=1)
        filtered = gain_re * own + gain_im * other
        zeros = jnp.zeros_like(filtered)
        split = jnp.concatenate([jnp.where(inside, filtered, zeros), jnp.where(inside, zeros, filtered)], axis=1)
        synthesis = jnp.dot(legendre, split.astype(jnp.bfloat16), preferred_element_type=jnp.float32)
        stage_ref[pair] = synthesis.astype(jnp.bfloat16)
        target = out_ref.at[order, pair]
        for turn in range(1, devices):
            peer = lax.rem(order + turn, devices)
            src = stage_ref.at[pair, pl.ds(peer * band, band)]
            to_order(src, target, send_sem.at[turn], recv_sem.at[turn], peer).start()
        pltpu.make_async_copy(stage_ref.at[pair, pl.ds(order * band, band)], target, own_sem).start()

        @pl.when(pair + 1 == early)
        def _():
            def gather(step, carry):
                line.step(step // groups + 1, step % groups)
                return carry

            lax.fori_loop((early - 1) // 2, steps, gather, 0)
            line.finish()
            l_copy(late_ref, 0, 1 - slot).start()

        @pl.when((pair + 1 < early) & (pair % 2 == 1) & (pair // 2 < steps))
        def _():
            step = pair // 2
            line.step(step // groups + 1, step % groups)

        return carry

    lax.fori_loop(0, pairs, body, 0)
    for turn in range(1, devices):
        peer = lax.rem(order + turn, devices)
        source = lax.rem(order + devices - turn, devices)
        both = to_order(out_ref.at[peer], out_ref.at[source], send_sem.at[turn], recv_sem.at[turn], peer)
        both.wait_send()
        both.wait_recv()
    pltpu.make_async_copy(out_ref.at[order], out_ref.at[order], own_sem).wait()


def inverse_kernel(scale_ref, band_ref, table_ref, out_ref, wide_ref):
    count, padded, lanes = band_ref.shape
    samples, steps, channels, longitudes = out_ref.shape
    sc = samples * channels
    block, part = pl.program_id(0), pl.program_id(1)

    @pl.when(part == 0)
    def _():
        def spread(pair, carry):
            wide_ref[pair] = band_ref[pair].astype(jnp.float32)
            return carry

        lax.fori_loop(0, count, spread, 0)

    pieces = []
    for t in range(steps):
        rows = wide_ref[:, part * steps + t].astype(jnp.bfloat16)
        pieces.append(jnp.concatenate([rows[:, q * sc : (q + 1) * sc] for q in range(4)], axis=0).T)
    values = jnp.dot(jnp.concatenate(pieces, axis=0), table_ref[...], preferred_element_type=jnp.float32)
    start = (block * pl.num_programs(1) + part) * steps
    for t in range(steps):
        scale = scale_ref[start + t]
        for s in range(samples):
            row = t * sc + s * channels
            out_ref[s, t] = (values[row : row + channels] * scale).astype(jnp.bfloat16)


def body(grad_out, legendre, filter_re, filter_im, quad_weight, pair_order, *, devices, members):
    samples, channels, lat_local, longitudes = grad_out.shape
    pairs, block_rows, packed_rows = legendre.shape
    lanes = 4 * samples * channels
    padded = -(-block_rows // TILE) * TILE
    per_band = lat_local // block_rows
    chips = members // 2
    columns = devices * pairs * 4
    early = (2 * pairs) // 3
    early_groups = step_of(early, 4)
    late_groups = step_of(pairs - early, 2)
    forward, inverse = basis_tables(pair_order)
    legendre = jnp.pad(legendre, ((0, 0), (0, padded - block_rows), (0, 0)))
    hbm = pl.BlockSpec(memory_space=pl.ANY)
    vmem = pl.BlockSpec(memory_space=pltpu.VMEM)
    smem = pl.BlockSpec(memory_space=pltpu.SMEM)
    bf16 = jnp.bfloat16
    dma = pltpu.SemaphoreType.DMA
    chunks = per_band * padded // TILE
    slack = max(0, (per_band - 1) * block_rows + padded - lat_local)

    def params(collective_id):
        return pltpu.CompilerParams(
            collective_id=collective_id, has_side_effects=True, vmem_limit_bytes=60 << 20
        )

    def line_sems(groups):
        return [dma((chips, groups)), dma((chips, groups)), dma((5,))]

    coeffs, early_table = pl.pallas_call(
        functools.partial(
            forward_kernel, devices=devices, chips=chips, groups=early_groups, block_rows=block_rows
        ),
        in_specs=[hbm, vmem, vmem],
        out_specs=[hbm, hbm],
        out_shape=[
            jax.ShapeDtypeStruct((pairs, members, padded, lanes), bf16),
            jax.ShapeDtypeStruct((early, members, padded, packed_rows), bf16),
        ],
        scratch_shapes=[
            pltpu.VMEM((2, samples, TILE + slack, channels, longitudes), bf16),
            pltpu.VMEM((TILE, columns, -(-(samples * channels) // 128) * 128), jnp.float32),
            pltpu.VMEM((chunks, devices * pairs, TILE, lanes), bf16),
            dma((2,)), dma((devices,)), dma((devices,)), dma, *line_sems(early_groups),
        ],
        compiler_params=params(0),
        name="fourier",
    )(jnp.transpose(grad_out, (0, 2, 1, 3)), forward, legendre)

    start_slot = lax.axis_index("order") * pairs
    low_order = lax.dynamic_slice_in_dim(pair_order, start_slot, pairs)
    both = jnp.concatenate([filter_re, filter_im], axis=0).T
    gains = jnp.pad(both, ((0, packed_rows), (0, 0)))
    tail = jnp.broadcast_to(both[M - 1 : M], (packed_rows - 1 - M, both.shape[1]))
    shifted = jnp.concatenate([both[:1], both, tail], axis=0)
    band, _ = pl.pallas_call(
        functools.partial(middle_kernel, devices=devices, chips=chips, groups=late_groups, samples=samples),
        in_specs=[smem, hbm, hbm, vmem, vmem, vmem],
        out_specs=[hbm, hbm],
        out_shape=[
            jax.ShapeDtypeStruct((devices, pairs, per_band * padded, lanes), bf16),
            jax.ShapeDtypeStruct((pairs - early, members, padded, packed_rows), bf16),
        ],
        scratch_shapes=[
            pltpu.VMEM((2, members, padded, lanes), bf16),
            pltpu.VMEM((2, members, padded, packed_rows), bf16),
            pltpu.VMEM((pairs, members * padded, lanes), bf16),
            dma((2,)), dma((2,)), dma((devices,)), dma((devices,)), dma, *line_sems(late_groups),
        ],
        compiler_params=params(1),
        name="legendre",
    )(low_order, coeffs, early_table, legendre, gains, shifted)

    scale = quad_weight * (2.0 * math.pi / NLON)
    steps = step_of(block_rows, 10)
    parts = block_rows // steps
    values = pl.pallas_call(
        inverse_kernel,
        grid=(per_band, parts),
        in_specs=[
            smem,
            pl.BlockSpec((devices * pairs, padded, lanes), lambda b, i: (0, b, 0)),
            pl.BlockSpec((columns, longitudes), lambda b, i: (0, 0)),
        ],
        out_specs=pl.BlockSpec((samples, steps, channels, longitudes), lambda b, i: (0, b * parts + i, 0, 0)),
        out_shape=jax.ShapeDtypeStruct((samples, lat_local, channels, longitudes), bf16),
        scratch_shapes=[pltpu.VMEM((devices * pairs, padded, lanes), jnp.float32)],
        compiler_params=pltpu.CompilerParams(
            dimension_semantics=("arbitrary", "arbitrary"), vmem_limit_bytes=56 << 20
        ),
        name="fourier_back",
    )(scale, band.reshape(devices * pairs, per_band * padded, lanes), inverse)
    return jnp.transpose(values, (0, 2, 1, 3))


def solution(mesh):
    in_specs = (
        P(None, "chan", "order", None),
        P("order", "chan", None),
        P("chan", None),
        P("chan", None),
        P("order"),
        P(),
    )
    out_specs = P(None, "chan", "order", None)
    local = functools.partial(body, devices=mesh.shape["order"], members=mesh.shape["chan"])
    return jax.shard_map(local, mesh=mesh, in_specs=in_specs, out_specs=out_specs, check_vma=False)
```

time: 374 us -> 233 us (0.62)
  waiting for transfers between devices: 160 us -> 0 us
  Pallas kernels: 92.2 us -> 209 us
  local copies, waits for them, and re-layouts: 44.1 us -> 7.25 us
  between operations: 36 us -> 0.09 us
  other arithmetic: 27.5 us -> 15.5 us
  starting transfers between devices: 11.9 us -> 0 us
    all_to_all x2 -> x0, waiting for transfers between devices: 153 us -> none  [the longest x1 89.4 us: body(): lax.all_to_all(synthesis, 'order', split_axis=0, concat_axis=0, tiled=True)]
    pallas_call x3, Pallas kernels: 92.2 us -> 209 us  [the longest x1 87.2 us: body(): pl.pallas_call(functools.partial(forward_kernel, devices=devices, chips=c...]
    unnamed x16 -> x4, local copies, waits for them, and re-layouts: 20.1 us -> 2.12 us
    all_gather x1 -> x0, local copies, waits for them, and re-layouts: 14.7 us -> none  [body(): whole = lax.all_gather(legendre, 'chan', axis=1, tiled=True)]
    all_to_all x2 -> x0, starting transfers between devices: 11.9 us -> none  [the longest x1 6.07 us: body(): lax.all_to_all(coeffs, 'order', split_axis=0, concat_axis=0, tiled=True)]
    unnamed x11 -> x0, other arithmetic: 10.3 us -> none
    all_gather x1 -> x0, waiting for transfers between devices: 7.24 us -> none  [body(): whole = lax.all_gather(legendre, 'chan', axis=1, tiled=True)]
    pad x2, local copies, waits for them, and re-layouts: 8.1 us -> 2.28 us  [the longest x1 1.36 us: body(): legendre = jnp.pad(legendre, ((0, 0), (0, padded - block_rows), (0, 0)))]
  transfers between devices with their start and end apart: 3 -> 0, of which waited for: 3 -> 0; matrix products, arithmetic and copies ran while one was open for 10% -> 0% of each run, Pallas kernels for 9% -> 0%
where the time goes in v1:
time: 233 us; the launch traced here: 232 us
  Pallas kernels  209 us (90%)
  other arithmetic  15.5 us (7%)
  local copies, waits for them, and re-layouts  7.25 us (3%)
    pallas_call x1, Pallas kernels, body(): pl.pallas_call(functools.partial(forward_kernel, devices=devices, chips=c...  87.2 us
    pallas_call x1, Pallas kernels, body(): pl.pallas_call(functools.partial(middle_kernel, devices=devices, chips=ch...  83.6 us
    pallas_call x1, Pallas kernels, body(): pl.pallas_call(inverse_kernel, grid=(per_band, parts), in_specs=[smem, pl...  38.7 us
    convert_element_type x1, other arithmetic, basis_tables(): inverse = inverse.astype(jnp.bfloat16).reshape(-1, 4, NLON)  6.29 us
    convert_element_type x1, other arithmetic, basis_tables(): forward = (inverse * factor[:, None]).astype(jnp.bfloat16)  5.55 us

profile of v1, /device:TPU:0, one launch (start us, length us, event | category | flops | bytes accessed | tf_op | source)
XLA Modules:
  0.0 232.3 jit_solution(15509275145601039234)
XLA Ops:
  0.0 1.3 dynamic_slice.3.low_ref
  1.3 0.7 subtract_bitcast_fusion
  2.0 1.3 broadcast_multiply_fusion.scale_ref
  3.2 0.1 rem.37
  3.3 0.7 fusion.12
  4.1 0.1 mul.68
  4.1 0.1 copy.10
  4.2 0.1 mul.59
  4.4 1.1 copy.12
  5.4 1.1 copy.13
  6.5 0.2 maximum_bitcast_fusion
  6.7 0.8 pad_maximum_fusion.shifted_ref
  7.5 0.9 pad.14.gains_ref
  8.4 5.6 %multiply_convert_fusion = bf16[192,1440]{1,0:T(8,128)(2,1)S(1)} fusion(f32[192]{0:T(256)S(1)} %compare_select_fusion, s32[192]{0:T(256)S(1)} %mul.59, pred[192]{0:T(512)(128)(4,1)S(1)} %fusion.10), kind=kLoop, calls=%fused_computation.10 | loop fusion | flops 3594240 | bytes 554688 | tf_op jit(solution)/shard_map/convert_element_type | solution.py:34
  14.0 0.1 pad_bitcast_fusion
  14.0 0.0 copy-start
  14.1 1.1 copy.11.table_ref
  15.2 6.3 %select_convert_fusion.table_ref = bf16[192,1440]{1,0:T(8,128)(2,1)} fusion(s32[192]{0:T(256)S(1)} %mul.68, pred[192]{0:T(512)(128)(4,1)S(1)} %fusion.11), kind=kLoop, calls=%fused_computation.6 | loop fusion | flops 3317760 | bytes 553920 | tf_op jit(solution)/shard_map/convert_element_type | solution.py:37
  21.5 0.0 copy-done
  21.5 1.4 pad.13.legendre_ref
  22.8 87.2 %fourier.1 = (bf16[12,8,96,384]{3,2,1,0:T(8,128)(2,1)}, bf16[8,8,96,768]{3,2,1,0:T(8,128)(2,1)}) custom-call(bf16[3,180,32,1440]{3,2,1,0:T(8,128)(2,1)} %bitcast.14, bf16[1440,256]{1,0:T(8,128)(2,1)} %copy.11.table_ref, bf16[12,96,768]{2,1,0:T(8,128)(2,1)} %pad.13.legendre_ref), custom_call_target="tpu_custom_call" | custom-call | tf_op jit(solution)/shard_map/fourier/pallas_call | solution.py:385
  110.0 83.6 %legendre.1 = (bf16[4,12,192,384]{3,2,1,0:T(8,128)(2,1)}, bf16[4,8,96,768]{3,2,1,0:T(8,128)(2,1)}) custom-call(s32[12]{0:T(128)} %dynamic_slice.3.low_ref, bf16[12,8,96,384]{3,2,1,0:T(8,128)(2,1)} %get-tuple-element.8.coeffs_ref, bf16[8,8,96,768]{3,2,1,0:T(8,128)(2,1)} %get-tuple-element.9.early_ref, bf16[12,96,768]{2,1,0:T(8,128)(2,1)} %pad.13.legendre_ref, ...), custom_call_target="tpu_custom_call" | custom-call | tf_op jit(solution)/shard_map/legendre/pallas_call | solution.py:411
  193.6 38.7 %fourier_back.1 = bf16[3,180,32,1440]{3,2,1,0:T(8,128)(2,1)} custom-call(f32[180]{0:T(256)} %broadcast_multiply_fusion.scale_ref, bf16[48,192,384]{2,1,0:T(8,128)(2,1)} %bitcast.15, bf16[192,1440]{1,0:T(8,128)(2,1)} %select_convert_fusion.table_ref), custom_call_target="tpu_custom_call" | custom-call | tf_op jit(solution)/shard_map/fourier_back/pallas_call | solution.py:432
  (6 shorter events, 0.0 us)
Async XLA Ops:
  14.0 7.4 %copy-start = (bf16[12,90,768]{2,1,0:T(8,128)(2,1)S(1)}, bf16[12,90,768]{2,1,0:T(8,128)(2,1)}, u32[]{:S(2)}) copy-start(bf16[12,90,768]{2,1,0:T(8,128)(2,1)} %param.7) | copy-start | bytes 4976644

commit v2 on v1

--- a/solution.py
+++ b/solution.py
@@ -11,6 +11,8 @@
 NLON = 1440
 M = 720
 TILE = 16
+FINE = 32
+HEAD = 8
 MESH = pl.DeviceIdType.MESH
 
 
@@ -18,24 +20,56 @@
     return max(d for d in range(1, most + 1) if count % d == 0)
 
 
-def basis_tables(pair_order):
-    low = pair_order
-    orders = jnp.stack([low, low, M - 1 - low, M - 1 - low], axis=1).reshape(-1)
-    columns = orders.shape[0]
-    real = jnp.arange(columns, dtype=jnp.int32) % 2 == 0
-    longitude = jnp.arange(NLON, dtype=jnp.int32)
-
-    def table(phases, real):
-        angles = (phases % NLON).astype(jnp.float32) * (2.0 * math.pi / NLON)
-        return jnp.where(real, jnp.cos(angles), -jnp.sin(angles))
-
-    inverse = table(orders[:, None] * longitude[None, :], real[:, None])
-    factor = jnp.where(orders == 0, 1.0, 2.0).astype(jnp.float32)
-    forward = (inverse * factor[:, None]).astype(jnp.bfloat16)
-    wide = -(-columns // 128) * 128
-    forward = jnp.pad(forward, ((0, wide - columns), (0, 0))).T
-    inverse = inverse.astype(jnp.bfloat16).reshape(-1, 4, NLON)
-    return forward, jnp.transpose(inverse, (1, 0, 2)).reshape(columns, NLON)
+def order_lanes(low_ref, sequence, width):
+    count = len(sequence)
+    lane = lax.broadcasted_iota(jnp.int32, (1, width), 1)
+    turn = sum((lane >= q * count).astype(jnp.int32) for q in range(1, 5))
+    place = lane - turn * count
+    low = jnp.zeros((1, width), jnp.float32)
+    for index, pair in enumerate(sequence):
+        low = jnp.where(place == index, low_ref[pair].astype(jnp.float32), low)
+    orders = jnp.where(turn < 2, low, (M - 1) - low)
+    return orders, (turn == 0) | (turn == 2), turn < 4
+
+
+def circle(phases):
+    phases = phases - NLON * jnp.floor(phases * (1.0 / NLON))
+    angles = phases * (2.0 * math.pi / NLON)
+    return jnp.cos(angles), jnp.sin(angles)
+
+
+def iota(shape, axis):
+    return lax.broadcasted_iota(jnp.int32, shape, axis).astype(jnp.float32)
+
+
+def fill_forward(low_ref, table_ref, count):
+    width = table_ref.shape[1]
+    orders, real, live = order_lanes(low_ref, range(count), width)
+    coarse_cos, coarse_sin = circle(iota((NLON // FINE, width), 0) * FINE * orders)
+    fine_cos, fine_sin = circle(iota((FINE, width), 0) * orders)
+    factor = jnp.where(orders == 0.0, 1.0, 2.0) * jnp.where(live, 1.0, 0.0)
+    first = jnp.where(real, coarse_cos, -coarse_sin) * factor
+    second = jnp.where(real, -coarse_sin, -coarse_cos) * factor
+    for part in range(NLON // FINE):
+        rows = first[part : part + 1] * fine_cos + second[part : part + 1] * fine_sin
+        table_ref[part * FINE : (part + 1) * FINE] = rows.astype(jnp.bfloat16)
+
+
+def fill_inverse(low_ref, table_ref, sequence):
+    columns = table_ref.shape[0]
+    width = -(-columns // 128) * 128
+    orders, real, _ = order_lanes(low_ref, sequence, width)
+    orders = jnp.broadcast_to(orders, (128, width)).T[:columns]
+    real = jnp.broadcast_to(jnp.where(real, 1.0, 0.0), (128, width)).T[:columns] > 0.5
+    fine_cos, fine_sin = circle(iota((columns, 128), 1) * orders)
+    coarse_cos, coarse_sin = circle(iota((columns, 128), 1) * 128.0 * orders)
+    first = jnp.where(real, coarse_cos, -coarse_sin)
+    second = jnp.where(real, -coarse_sin, -coarse_cos)
+    for start in range(0, NLON, 128):
+        part = start // 128
+        values = first[:, part : part + 1] * fine_cos + second[:, part : part + 1] * fine_sin
+        size = min(128, NLON - start)
+        table_ref[:, start : start + size] = values[:, :size].astype(jnp.bfloat16)
 
 
 class Line:
@@ -150,7 +184,7 @@
 
 
 def forward_kernel(
-    x_ref, table_ref, legendre_ref, out_ref, gathered_ref, x_buf, turned_ref, stage_ref,
+    low_ref, x_ref, legendre_ref, out_ref, gathered_ref, x_buf, table_ref, turned_ref, stage_ref,
     x_sem, send_sem, recv_sem, own_sem, up_sem, down_sem, flag_sem, *, devices, chips, groups, block_rows
 ):
     samples, lat_local, channels, _ = x_ref.shape
@@ -175,6 +209,8 @@
     enter(devices, chips)
     line.start()
     steps = (chips - 1) * groups
+    count = devices * pairs
+    fill_forward(low_ref, table_ref, count)
 
     def body(chunk, carry):
         slot = chunk % 2
@@ -191,8 +227,8 @@
             turned_ref[t, :, 0:sc] = turned[: turned_ref.shape[1]]
         block, part = chunk // per_block, chunk % per_block
         live = lax.broadcasted_iota(jnp.int32, (TILE, lanes), 0) < block_rows - part * TILE
-        for pair in range(devices * pairs):
-            row = jnp.concatenate([turned_ref[:, 4 * pair + q, 0:sc] for q in range(4)], axis=1)
+        for pair in range(count):
+            row = jnp.concatenate([turned_ref[:, q * count + pair, 0:sc] for q in range(4)], axis=1)
             stage_ref[chunk, pair] = jnp.where(live, row, 0.0).astype(jnp.bfloat16)
         target = out_ref.at[:, order * per_band + block, pl.ds(part * TILE, TILE)]
         for turn in range(1, devices):
@@ -230,8 +266,10 @@
 
 
 def middle_kernel(
-    low_ref, coeffs_ref, early_ref, legendre_ref, gains_ref, shifted_ref, out_ref, late_ref, z_buf, l_buf, stage_ref,
-    z_sem, l_sem, send_sem, recv_sem, own_sem, up_sem, down_sem, flag_sem, *, devices, chips, groups, samples
+    low_ref, coeffs_ref, early_ref, legendre_ref, filter_re_ref, filter_im_ref, out_ref, inverse_ref, late_ref,
+    z_buf, l_buf, gains_ref, stage_ref, band_buf, wide_ref, rows_buf,
+    z_sem, l_sem, send_sem, recv_sem, own_sem, out_sem, up_sem, down_sem, flag_sem,
+    *, devices, chips, groups, samples, sequence
 ):
     pairs, blocks, padded, lanes = coeffs_ref.shape
     packed_rows = legendre_ref.shape[2]
@@ -255,6 +293,13 @@
     enter(devices, chips)
     line.start()
     steps = (chips - 1) * groups
+    sets, share, lat_local = out_ref.shape[0], out_ref.shape[2] // devices, out_ref.shape[1]
+    degrees = filter_re_ref.shape[1]
+    filters = jnp.concatenate([filter_re_ref[...], filter_im_ref[...]], axis=0)
+    filters = jnp.concatenate([filters, jnp.zeros((2 * channels, packed_rows - degrees), jnp.float32)], axis=1).T
+    gains_ref[HEAD : HEAD + packed_rows] = filters
+    gains_ref[HEAD + packed_rows :] = jnp.zeros((degrees, 2 * channels), jnp.float32)
+    gains_ref[HEAD - 1 : HEAD] = filters[0:1]
     contract = (((0,), (0,)), ((), ()))
     row_ids = lax.broadcasted_iota(jnp.int32, (packed_rows, half), 0)
 
@@ -278,11 +323,12 @@
         legendre = l_buf[slot].reshape(rows, packed_rows)
         coeffs = z_buf[slot].reshape(rows, lanes)
         spectrum = lax.dot_general(legendre, coeffs, contract, preferred_element_type=jnp.float32)
-        low = low_ref[pair]
+        low = low_ref[order * pairs + pair]
         inside = row_ids < M - low
         own = jnp.where(inside, spectrum[:, :half], spectrum[:, half:])
         other = jnp.concatenate([own[:, sc:], own[:, :sc]], axis=1)
-        gains = jnp.where(inside[:, : 2 * channels], gains_ref[pl.ds(low, packed_rows), :], shifted_ref[...])
+        upper = gains_ref[pl.ds(low + HEAD, packed_rows), :]
+        gains = jnp.where(inside[:, : 2 * channels], upper, gains_ref[pl.ds(HEAD - 1, packed_rows), :])
         gain_re = gains[:, :channels]
         gain_im = gains[:, channels:]
         gain_re = jnp.concatenate([gain_re] * (2 * samples), axis=1)
@@ -292,12 +338,13 @@
         split = jnp.concatenate([jnp.where(inside, filtered, zeros), jnp.where(inside, zeros, filtered)], axis=1)
         synthesis = jnp.dot(legendre, split.astype(jnp.bfloat16), preferred_element_type=jnp.float32)
         stage_ref[pair] = synthesis.astype(jnp.bfloat16)
-        target = out_ref.at[order, pair]
+        bundle = pair // share
+        target = band_buf.at[bundle, order, pair % share]
         for turn in range(1, devices):
             peer = lax.rem(order + turn, devices)
             src = stage_ref.at[pair, pl.ds(peer * band, band)]
-            to_order(src, target, send_sem.at[turn], recv_sem.at[turn], peer).start()
-        pltpu.make_async_copy(stage_ref.at[pair, pl.ds(order * band, band)], target, own_sem).start()
+            to_order(src, target, send_sem.at[turn], recv_sem.at[turn, bundle], peer).start()
+        pltpu.make_async_copy(stage_ref.at[pair, pl.ds(order * band, band)], target, own_sem.at[bundle]).start()
 
         @pl.when(pair + 1 == early)
         def _():
@@ -317,37 +364,53 @@
         return carry
 
     lax.fori_loop(0, pairs, body, 0)
+    fill_inverse(low_ref, inverse_ref, sequence)
+    block_rows = lat_local // (blocks // devices)
+
+    def rows_copy(bundle):
+        return pltpu.make_async_copy(rows_buf.at[bundle], out_ref.at[bundle], out_sem.at[bundle])
+
+    def spread(bundle, carry):
+        for turn in range(1, devices):
+            source = lax.rem(order + devices - turn, devices)
+            got = band_buf.at[bundle, source]
+            to_order(got, got, send_sem.at[turn], recv_sem.at[turn, bundle], source).wait_recv()
+        got = band_buf.at[bundle, order]
+        pltpu.make_async_copy(got, got, own_sem.at[bundle]).wait()
+        for device in range(devices):
+            for entry in range(share):
+                wide_ref[device * share + entry] = band_buf[bundle, device, entry].astype(jnp.float32)
+
+        def turn_row(lat, carry):
+            row = (lat // block_rows) * padded + lat % block_rows
+            rows_buf[bundle, lat] = wide_ref[:, row].astype(jnp.bfloat16)
+            return carry
+
+        lax.fori_loop(0, lat_local, turn_row, 0, unroll=step_of(lat_local, 10))
+        rows_copy(bundle).start()
+        return carry
+
+    lax.fori_loop(0, sets, spread, 0)
     for turn in range(1, devices):
         peer = lax.rem(order + turn, devices)
-        source = lax.rem(order + devices - turn, devices)
-        both = to_order(out_ref.at[peer], out_ref.at[source], send_sem.at[turn], recv_sem.at[turn], peer)
-        both.wait_send()
-        both.wait_recv()
-    pltpu.make_async_copy(out_ref.at[order], out_ref.at[order], own_sem).wait()
-
-
-def inverse_kernel(scale_ref, band_ref, table_ref, out_ref, wide_ref):
-    count, padded, lanes = band_ref.shape
-    samples, steps, channels, longitudes = out_ref.shape
+        sent = stage_ref.at[:, pl.ds(peer * band, band)]
+        to_order(sent, sent, send_sem.at[turn], recv_sem.at[turn, 0], peer).wait_send()
+    for bundle in range(sets):
+        rows_copy(bundle).wait()
+
+
+def inverse_kernel(weight_ref, band_ref, table_ref, out_ref):
+    sets, steps, _, lanes = band_ref.shape
+    samples, _, channels, _ = out_ref.shape
     sc = samples * channels
-    block, part = pl.program_id(0), pl.program_id(1)
-
-    @pl.when(part == 0)
-    def _():
-        def spread(pair, carry):
-            wide_ref[pair] = band_ref[pair].astype(jnp.float32)
-            return carry
-
-        lax.fori_loop(0, count, spread, 0)
-
     pieces = []
     for t in range(steps):
-        rows = wide_ref[:, part * steps + t].astype(jnp.bfloat16)
+        rows = jnp.concatenate([band_ref[g, t] for g in range(sets)], axis=0)
         pieces.append(jnp.concatenate([rows[:, q * sc : (q + 1) * sc] for q in range(4)], axis=0).T)
     values = jnp.dot(jnp.concatenate(pieces, axis=0), table_ref[...], preferred_element_type=jnp.float32)
-    start = (block * pl.num_programs(1) + part) * steps
+    start = pl.program_id(0) * steps
     for t in range(steps):
-        scale = scale_ref[start + t]
+        scale = weight_ref[start + t] * (2.0 * math.pi / NLON)
         for s in range(samples):
             row = t * sc + s * channels
             out_ref[s, t] = (values[row : row + channels] * scale).astype(jnp.bfloat16)
@@ -364,7 +427,6 @@
     early = (2 * pairs) // 3
     early_groups = step_of(early, 4)
     late_groups = step_of(pairs - early, 2)
-    forward, inverse = basis_tables(pair_order)
     legendre = jnp.pad(legendre, ((0, 0), (0, padded - block_rows), (0, 0)))
     hbm = pl.BlockSpec(memory_space=pl.ANY)
     vmem = pl.BlockSpec(memory_space=pltpu.VMEM)
@@ -386,7 +448,7 @@
         functools.partial(
             forward_kernel, devices=devices, chips=chips, groups=early_groups, block_rows=block_rows
         ),
-        in_specs=[hbm, vmem, vmem],
+        in_specs=[smem, hbm, vmem],
         out_specs=[hbm, hbm],
         out_shape=[
             jax.ShapeDtypeStruct((pairs, members, padded, lanes), bf16),
@@ -394,57 +456,61 @@
         ],
         scratch_shapes=[
             pltpu.VMEM((2, samples, TILE + slack, channels, longitudes), bf16),
+            pltpu.VMEM((longitudes, -(-columns // 128) * 128), bf16),
             pltpu.VMEM((TILE, columns, -(-(samples * channels) // 128) * 128), jnp.float32),
             pltpu.VMEM((chunks, devices * pairs, TILE, lanes), bf16),
             dma((2,)), dma((devices,)), dma((devices,)), dma, *line_sems(early_groups),
         ],
         compiler_params=params(0),
         name="fourier",
-    )(jnp.transpose(grad_out, (0, 2, 1, 3)), forward, legendre)
-
-    start_slot = lax.axis_index("order") * pairs
-    low_order = lax.dynamic_slice_in_dim(pair_order, start_slot, pairs)
-    both = jnp.concatenate([filter_re, filter_im], axis=0).T
-    gains = jnp.pad(both, ((0, packed_rows), (0, 0)))
-    tail = jnp.broadcast_to(both[M - 1 : M], (packed_rows - 1 - M, both.shape[1]))
-    shifted = jnp.concatenate([both[:1], both, tail], axis=0)
-    band, _ = pl.pallas_call(
-        functools.partial(middle_kernel, devices=devices, chips=chips, groups=late_groups, samples=samples),
+    )(pair_order, jnp.transpose(grad_out, (0, 2, 1, 3)), legendre)
+
+    share = step_of(pairs, 4)
+    sets = pairs // share
+    sequence = [d * pairs + g * share + j for g in range(sets) for d in range(devices) for j in range(share)]
+    rows = per_band * padded
+    band, inverse, _ = pl.pallas_call(
+        functools.partial(
+            middle_kernel, devices=devices, chips=chips, groups=late_groups, samples=samples, sequence=sequence
+        ),
         in_specs=[smem, hbm, hbm, vmem, vmem, vmem],
-        out_specs=[hbm, hbm],
+        out_specs=[hbm, vmem, hbm],
         out_shape=[
-            jax.ShapeDtypeStruct((devices, pairs, per_band * padded, lanes), bf16),
+            jax.ShapeDtypeStruct((sets, lat_local, devices * share, lanes), bf16),
+            jax.ShapeDtypeStruct((columns, longitudes), bf16),
             jax.ShapeDtypeStruct((pairs - early, members, padded, packed_rows), bf16),
         ],
         scratch_shapes=[
             pltpu.VMEM((2, members, padded, lanes), bf16),
             pltpu.VMEM((2, members, padded, packed_rows), bf16),
+            pltpu.VMEM((HEAD + packed_rows + filter_re.shape[1], 2 * channels), jnp.float32),
             pltpu.VMEM((pairs, members * padded, lanes), bf16),
-            dma((2,)), dma((2,)), dma((devices,)), dma((devices,)), dma, *line_sems(late_groups),
+            pltpu.VMEM((sets, devices, share, rows, lanes), bf16),
+            pltpu.VMEM((devices * share, rows, lanes), jnp.float32),
+            pltpu.VMEM((sets, lat_local, devices * share, lanes), bf16),
+            dma((2,)), dma((2,)), dma((devices,)), dma((devices, sets)), dma((sets,)), dma((sets,)),
+            *line_sems(late_groups),
         ],
         compiler_params=params(1),
         name="legendre",
-    )(low_order, coeffs, early_table, legendre, gains, shifted)
-
-    scale = quad_weight * (2.0 * math.pi / NLON)
-    steps = step_of(block_rows, 10)
-    parts = block_rows // steps
+    )(pair_order, coeffs, early_table, legendre, filter_re, filter_im)
+
+    steps = step_of(lat_local, 20)
     values = pl.pallas_call(
         inverse_kernel,
-        grid=(per_band, parts),
+        grid=(lat_local // steps,),
         in_specs=[
             smem,
-            pl.BlockSpec((devices * pairs, padded, lanes), lambda b, i: (0, b, 0)),
-            pl.BlockSpec((columns, longitudes), lambda b, i: (0, 0)),
+            pl.BlockSpec((sets, steps, devices * share, lanes), lambda i: (0, i, 0, 0)),
+            pl.BlockSpec((columns, longitudes), lambda i: (0, 0)),
         ],
-        out_specs=pl.BlockSpec((samples, steps, channels, longitudes), lambda b, i: (0, b * parts + i, 0, 0)),
+        out_specs=pl.BlockSpec((samples, steps, channels, longitudes), lambda i: (0, i, 0, 0)),
         out_shape=jax.ShapeDtypeStruct((samples, lat_local, channels, longitudes), bf16),
-        scratch_shapes=[pltpu.VMEM((devices * pairs, padded, lanes), jnp.float32)],
         compiler_params=pltpu.CompilerParams(
-            dimension_semantics=("arbitrary", "arbitrary"), vmem_limit_bytes=56 << 20
+            dimension_semantics=("arbitrary",), vmem_limit_bytes=56 << 20
         ),
         name="fourier_back",
-    )(scale, band.reshape(devices * pairs, per_band * padded, lanes), inverse)
+    )(quad_weight, band, inverse)
     return jnp.transpose(values, (0, 2, 1, 3))
 
 

time: 233 us -> 207 us (0.89)
  other arithmetic: 15.5 us -> 0 us
  Pallas kernels: 209 us -> 204 us
  local copies, waits for them, and re-layouts: 7.25 us -> 2.83 us
    pallas_call x1, Pallas kernels: 38.7 us -> 26.5 us  [body(): pl.pallas_call(inverse_kernel, grid=(lat_local // steps,), in_specs=[smem...]
    convert_element_type x2 -> x0, other arithmetic: 11.8 us -> none  [the longest x1 6.29 us: basis_tables(): inverse = inverse.astype(jnp.bfloat16).reshape(-1, 4, NLON)]
    pallas_call x1, Pallas kernels: 83.6 us -> 90.5 us  [body(): pl.pallas_call(functools.partial(middle_kernel, devices=devices, chips=ch...]
where the time goes in v2:
time: 207 us
  Pallas kernels  204 us (99%)
  local copies, waits for them, and re-layouts  2.83 us (1%)
    pallas_call x1, Pallas kernels, body(): pl.pallas_call(functools.partial(middle_kernel, devices=devices, chips=ch...  90.5 us
    pallas_call x1, Pallas kernels, body(): pl.pallas_call(functools.partial(forward_kernel, devices=devices, chips=c...  86.8 us
    pallas_call x1, Pallas kernels, body(): pl.pallas_call(inverse_kernel, grid=(lat_local // steps,), in_specs=[smem...  26.5 us

profile of v2, /device:TPU:0, one launch (start us, length us, event | category | flops | bytes accessed | tf_op | source)
XLA Modules:
  0.0 206.7 jit_solution(12624973494284664837)
XLA Ops:
  0.0 2.8 %pad.4.legendre_ref = bf16[12,96,768]{2,1,0:T(8,128)(2,1)} pad(bf16[12,90,768]{2,1,0:T(8,128)(2,1)} %param.7, bf16[]{:T(256)} %constant.2.clone.1), padding=0_0x0_6x0_0 | pad | bytes 3428354 | tf_op jit(solution)/shard_map/jit(_pad)/pad | solution.py:430
  2.8 86.8 %fourier.1 = (bf16[12,8,96,384]{3,2,1,0:T(8,128)(2,1)}, bf16[8,8,96,768]{3,2,1,0:T(8,128)(2,1)}) custom-call(s32[48]{0:T(128)} %low_ref.3, bf16[3,180,32,1440]{3,2,1,0:T(8,128)(2,1)} %bitcast.2, bf16[12,96,768]{2,1,0:T(8,128)(2,1)} %pad.4.legendre_ref), custom_call_target="tpu_custom_call" | custom-call | tf_op jit(solution)/shard_map/fourier/pallas_call | solution.py:447
  89.7 90.5 %legendre.1 = (bf16[3,180,16,384]{3,2,1,0:T(8,128)(2,1)}, bf16[192,1440]{1,0:T(8,128)(2,1)}, bf16[4,8,96,768]{3,2,1,0:T(8,128)(2,1)}) custom-call(s32[48]{0:T(128)} %low_ref.3, bf16[12,8,96,384]{3,2,1,0:T(8,128)(2,1)} %get-tuple-element.9.coeffs_ref, bf16[8,8,96,768]{3,2,1,0:T(8,128)(2,1)} %get-tuple-element.10.early_ref, ...), custom_call_target="tpu_custom_call" | custom-call | tf_op jit(solution)/shard_map/legendre/pallas_call | solution.py:472
  180.2 26.5 %fourier_back.1 = bf16[3,180,32,1440]{3,2,1,0:T(8,128)(2,1)} custom-call(f32[180]{0:T(256)} %weight_ref.1, bf16[3,180,16,384]{3,2,1,0:T(8,128)(2,1)} %get-tuple-element.11.band_ref, bf16[192,1440]{1,0:T(8,128)(2,1)} %get-tuple-element.12.table_ref), custom_call_target="tpu_custom_call" | custom-call | tf_op jit(solution)/shard_map/fourier_back/pallas_call | solution.py:499

commit v3 on v2

--- a/solution.py
+++ b/solution.py
@@ -266,9 +266,9 @@
 
 
 def middle_kernel(
-    low_ref, coeffs_ref, early_ref, legendre_ref, filter_re_ref, filter_im_ref, out_ref, inverse_ref, late_ref,
-    z_buf, l_buf, gains_ref, stage_ref, band_buf, wide_ref, rows_buf,
-    z_sem, l_sem, send_sem, recv_sem, own_sem, out_sem, up_sem, down_sem, flag_sem,
+    low_ref, coeffs_ref, early_ref, legendre_ref, filter_re_ref, filter_im_ref,
+    out_ref, last_ref, rest_ref, inverse_ref, late_ref, z_buf, l_buf, gains_ref, stage_ref, band_buf, wide_ref, rows_buf,
+    z_sem, l_sem, send_sem, recv_sem, own_sem, out_sem, rest_sem, up_sem, down_sem, flag_sem,
     *, devices, chips, groups, samples, sequence
 ):
     pairs, blocks, padded, lanes = coeffs_ref.shape
@@ -293,7 +293,8 @@
     enter(devices, chips)
     line.start()
     steps = (chips - 1) * groups
-    sets, share, lat_local = out_ref.shape[0], out_ref.shape[2] // devices, out_ref.shape[1]
+    sets, share, lat_local = out_ref.shape[0] + 1, out_ref.shape[2] // devices, out_ref.shape[1]
+    head = band - padded
     degrees = filter_re_ref.shape[1]
     filters = jnp.concatenate([filter_re_ref[...], filter_im_ref[...]], axis=0)
     filters = jnp.concatenate([filters, jnp.zeros((2 * channels, packed_rows - degrees), jnp.float32)], axis=1).T
@@ -339,12 +340,26 @@
         synthesis = jnp.dot(legendre, split.astype(jnp.bfloat16), preferred_element_type=jnp.float32)
         stage_ref[pair] = synthesis.astype(jnp.bfloat16)
         bundle = pair // share
-        target = band_buf.at[bundle, order, pair % share]
-        for turn in range(1, devices):
-            peer = lax.rem(order + turn, devices)
-            src = stage_ref.at[pair, pl.ds(peer * band, band)]
-            to_order(src, target, send_sem.at[turn], recv_sem.at[turn, bundle], peer).start()
-        pltpu.make_async_copy(stage_ref.at[pair, pl.ds(order * band, band)], target, own_sem.at[bundle]).start()
+
+        def send(size, part):
+            target = band_buf.at[bundle, order, pair % share, pl.ds(0, size)]
+            for turn in range(1, devices):
+                peer = lax.rem(order + turn, devices)
+                src = stage_ref.at[pair, pl.ds(peer * band, size)]
+                to_order(src, target, send_sem.at[turn, part], recv_sem.at[turn, bundle], peer).start()
+            src = stage_ref.at[pair, pl.ds(order * band, size)]
+            pltpu.make_async_copy(src, target, own_sem.at[bundle]).start()
+
+        @pl.when(bundle < sets - 1)
+        def _():
+            send(band, 0)
+
+        @pl.when(bundle == sets - 1)
+        def _():
+            send(head, 1)
+            for device in range(devices):
+                src = stage_ref.at[pair, pl.ds(device * band + head, padded)]
+                pltpu.make_async_copy(src, rest_ref.at[device, pair % share], rest_sem).start()
 
         @pl.when(pair + 1 == early)
         def _():
@@ -366,54 +381,87 @@
     lax.fori_loop(0, pairs, body, 0)
     fill_inverse(low_ref, inverse_ref, sequence)
     block_rows = lat_local // (blocks // devices)
+    early_lat = lat_local - block_rows
 
     def rows_copy(bundle):
+        if bundle is None:
+            return pltpu.make_async_copy(rows_buf.at[sets - 1, pl.ds(0, early_lat)], last_ref, out_sem.at[sets - 1])
         return pltpu.make_async_copy(rows_buf.at[bundle], out_ref.at[bundle], out_sem.at[bundle])
 
-    def spread(bundle, carry):
+    def spread(bundle, size, lats):
         for turn in range(1, devices):
             source = lax.rem(order + devices - turn, devices)
-            got = band_buf.at[bundle, source]
-            to_order(got, got, send_sem.at[turn], recv_sem.at[turn, bundle], source).wait_recv()
-        got = band_buf.at[bundle, order]
+            got = band_buf.at[bundle, source, :, pl.ds(0, size)]
+            to_order(got, got, send_sem.at[turn, 0], recv_sem.at[turn, bundle], source).wait_recv()
+        got = band_buf.at[bundle, order, :, pl.ds(0, size)]
         pltpu.make_async_copy(got, got, own_sem.at[bundle]).wait()
         for device in range(devices):
             for entry in range(share):
-                wide_ref[device * share + entry] = band_buf[bundle, device, entry].astype(jnp.float32)
+                wide_ref[device * share + entry, 0:size] = band_buf[bundle, device, entry, 0:size].astype(jnp.float32)
 
         def turn_row(lat, carry):
             row = (lat // block_rows) * padded + lat % block_rows
             rows_buf[bundle, lat] = wide_ref[:, row].astype(jnp.bfloat16)
             return carry
 
-        lax.fori_loop(0, lat_local, turn_row, 0, unroll=step_of(lat_local, 10))
+        lax.fori_loop(0, lats, turn_row, 0, unroll=step_of(lats, 10))
+
+    def whole(bundle, carry):
+        spread(bundle, band, lat_local)
         rows_copy(bundle).start()
         return carry
 
-    lax.fori_loop(0, sets, spread, 0)
+    lax.fori_loop(0, sets - 1, whole, 0)
+    spread(sets - 1, head, early_lat)
+    rows_copy(None).start()
+    full = pairs - share
     for turn in range(1, devices):
         peer = lax.rem(order + turn, devices)
-        sent = stage_ref.at[:, pl.ds(peer * band, band)]
-        to_order(sent, sent, send_sem.at[turn], recv_sem.at[turn, 0], peer).wait_send()
-    for bundle in range(sets):
+        sent = stage_ref.at[pl.ds(0, full), pl.ds(peer * band, band)]
+        to_order(sent, sent, send_sem.at[turn, 0], recv_sem.at[turn, 0], peer).wait_send()
+        sent = stage_ref.at[pl.ds(full, share), pl.ds(peer * band, head)]
+        to_order(sent, sent, send_sem.at[turn, 1], recv_sem.at[turn, 0], peer).wait_send()
+    pltpu.make_async_copy(rest_ref, rest_ref, rest_sem).wait()
+    for bundle in range(sets - 1):
         rows_copy(bundle).wait()
-
-
-def inverse_kernel(weight_ref, band_ref, table_ref, out_ref):
-    sets, steps, _, lanes = band_ref.shape
-    samples, _, channels, _ = out_ref.shape
+    rows_copy(None).wait()
+
+
+def emit(row_sets, start, weight_ref, table_ref, out_ref):
+    samples, steps, channels, _ = out_ref.shape
     sc = samples * channels
     pieces = []
     for t in range(steps):
-        rows = jnp.concatenate([band_ref[g, t] for g in range(sets)], axis=0)
+        rows = jnp.concatenate([part(t) for part in row_sets], axis=0)
         pieces.append(jnp.concatenate([rows[:, q * sc : (q + 1) * sc] for q in range(4)], axis=0).T)
     values = jnp.dot(jnp.concatenate(pieces, axis=0), table_ref[...], preferred_element_type=jnp.float32)
-    start = pl.program_id(0) * steps
     for t in range(steps):
         scale = weight_ref[start + t] * (2.0 * math.pi / NLON)
         for s in range(samples):
             row = t * sc + s * channels
             out_ref[s, t] = (values[row : row + channels] * scale).astype(jnp.bfloat16)
+
+
+def first_kernel(weight_ref, band_ref, last_ref, table_ref, out_ref):
+    row_sets = [functools.partial(lambda g, t: band_ref[g, t], g) for g in range(band_ref.shape[0])]
+    row_sets.append(lambda t: last_ref[t])
+    emit(row_sets, pl.program_id(0) * out_ref.shape[1], weight_ref, table_ref, out_ref)
+
+
+def second_kernel(weight_ref, band_ref, rest_ref, table_ref, _, out_ref, wide_ref, *, offset):
+    steps = out_ref.shape[1]
+    part = pl.program_id(0)
+
+    @pl.when(part == 0)
+    def _():
+        devices, share, _, _ = rest_ref.shape
+        for device in range(devices):
+            for entry in range(share):
+                wide_ref[device * share + entry] = rest_ref[device, entry].astype(jnp.float32)
+
+    row_sets = [functools.partial(lambda g, t: band_ref[g, t], g) for g in range(band_ref.shape[0])]
+    row_sets.append(lambda t: wide_ref[:, part * steps + t].astype(jnp.bfloat16))
+    emit(row_sets, offset + part * steps, weight_ref, table_ref, out_ref)
 
 
 def body(grad_out, legendre, filter_re, filter_im, quad_weight, pair_order, *, devices, members):
@@ -469,14 +517,16 @@
     sets = pairs // share
     sequence = [d * pairs + g * share + j for g in range(sets) for d in range(devices) for j in range(share)]
     rows = per_band * padded
-    band, inverse, _ = pl.pallas_call(
+    band, last, rest, inverse, _ = pl.pallas_call(
         functools.partial(
             middle_kernel, devices=devices, chips=chips, groups=late_groups, samples=samples, sequence=sequence
         ),
         in_specs=[smem, hbm, hbm, vmem, vmem, vmem],
-        out_specs=[hbm, vmem, hbm],
+        out_specs=[hbm, hbm, hbm, vmem, hbm],
         out_shape=[
-            jax.ShapeDtypeStruct((sets, lat_local, devices * share, lanes), bf16),
+            jax.ShapeDtypeStruct((sets - 1, lat_local, devices * share, lanes), bf16),
+            jax.ShapeDtypeStruct((lat_local - block_rows, devices * share, lanes), bf16),
+            jax.ShapeDtypeStruct((devices, share, padded, lanes), bf16),
             jax.ShapeDtypeStruct((columns, longitudes), bf16),
             jax.ShapeDtypeStruct((pairs - early, members, padded, packed_rows), bf16),
         ],
@@ -488,29 +538,61 @@
             pltpu.VMEM((sets, devices, share, rows, lanes), bf16),
             pltpu.VMEM((devices * share, rows, lanes), jnp.float32),
             pltpu.VMEM((sets, lat_local, devices * share, lanes), bf16),
-            dma((2,)), dma((2,)), dma((devices,)), dma((devices, sets)), dma((sets,)), dma((sets,)),
+            dma((2,)), dma((2,)), dma((devices, 2)), dma((devices, sets)), dma((sets,)), dma((sets,)), dma,
             *line_sems(late_groups),
         ],
         compiler_params=params(1),
         name="legendre",
     )(pair_order, coeffs, early_table, legendre, filter_re, filter_im)
 
-    steps = step_of(lat_local, 20)
+    rest = lax.all_to_all(rest, "order", split_axis=0, concat_axis=0, tiled=True)
+    steps = step_of(block_rows, 18)
+    early_lat = lat_local - block_rows
+    ahead = early_lat // steps
+    shape = jax.ShapeDtypeStruct((samples, lat_local, channels, longitudes), bf16)
+    plain = pltpu.CompilerParams(dimension_semantics=("arbitrary",), vmem_limit_bytes=56 << 20)
+    table_block = pl.BlockSpec((columns, longitudes), lambda i: (0, 0))
+
+    def cost(lats):
+        return pl.CostEstimate(
+            flops=2 * lats * samples * channels * columns * longitudes,
+            bytes_accessed=2 * lats * samples * channels * (columns + longitudes),
+            transcendentals=0,
+        )
+
     values = pl.pallas_call(
-        inverse_kernel,
-        grid=(lat_local // steps,),
+        first_kernel,
+        grid=(ahead,),
         in_specs=[
             smem,
-            pl.BlockSpec((sets, steps, devices * share, lanes), lambda i: (0, i, 0, 0)),
-            pl.BlockSpec((columns, longitudes), lambda i: (0, 0)),
+            pl.BlockSpec((sets - 1, steps, devices * share, lanes), lambda i: (0, i, 0, 0)),
+            pl.BlockSpec((steps, devices * share, lanes), lambda i: (i, 0, 0)),
+            table_block,
         ],
         out_specs=pl.BlockSpec((samples, steps, channels, longitudes), lambda i: (0, i, 0, 0)),
-        out_shape=jax.ShapeDtypeStruct((samples, lat_local, channels, longitudes), bf16),
-        compiler_params=pltpu.CompilerParams(
-            dimension_semantics=("arbitrary",), vmem_limit_bytes=56 << 20
-        ),
+        out_shape=shape,
+        compiler_params=plain,
+        cost_estimate=cost(early_lat),
         name="fourier_back",
-    )(quad_weight, band, inverse)
+    )(quad_weight, band, last, inverse)
+    values = pl.pallas_call(
+        functools.partial(second_kernel, offset=early_lat),
+        grid=(block_rows // steps,),
+        in_specs=[
+            smem,
+            pl.BlockSpec((sets - 1, steps, devices * share, lanes), lambda i: (0, ahead + i, 0, 0)),
+            vmem,
+            table_block,
+            hbm,
+        ],
+        out_specs=pl.BlockSpec((samples, steps, channels, longitudes), lambda i: (0, ahead + i, 0, 0)),
+        out_shape=shape,
+        scratch_shapes=[pltpu.VMEM((devices * share, padded, lanes), jnp.float32)],
+        input_output_aliases={4: 0},
+        compiler_params=plain,
+        cost_estimate=cost(block_rows),
+        name="fourier_back_rest",
+    )(quad_weight, band, rest, inverse, values)
     return jnp.transpose(values, (0, 2, 1, 3))
 
 

time: 207 us -> 201 us (0.971)
  Pallas kernels: 204 us -> 193 us
  starting transfers between devices: 0 us -> 3.72 us
    pallas_call x1, Pallas kernels: 90.5 us -> 75.2 us  [body(): pl.pallas_call(functools.partial(middle_kernel, devices=devices, chips=ch...]
    pallas_call x1 -> x2, Pallas kernels: 26.5 us -> 31.1 us  [the longest x1 15.8 us: body(): pl.pallas_call(functools.partial(second_kernel, offset=early_lat), grid=(...]
    all_to_all x0 -> x1, starting transfers between devices: none -> 3.72 us  [body(): lax.all_to_all(rest, 'order', split_axis=0, concat_axis=0, tiled=True)]
  transfers between devices with their start and end apart: 0 -> 1, of which waited for: 0 -> 0; matrix products, arithmetic and copies ran while one was open for 0% -> 0% of each run, Pallas kernels for 0% -> 8%
where the time goes in v3:
time: 201 us
  Pallas kernels  193 us (96%)
  local copies, waits for them, and re-layouts  3.88 us (2%)
  starting transfers between devices  3.72 us (2%)
    pallas_call x1, Pallas kernels, body(): pl.pallas_call(functools.partial(forward_kernel, devices=devices, chips=c...  86.8 us
    pallas_call x1, Pallas kernels, body(): pl.pallas_call(functools.partial(middle_kernel, devices=devices, chips=ch...  75.2 us
    pallas_call x1, Pallas kernels, body(): pl.pallas_call(functools.partial(second_kernel, offset=early_lat), grid=(...  15.8 us
    pallas_call x1, Pallas kernels, body(): pl.pallas_call(first_kernel, grid=(ahead,), in_specs=[smem, pl.BlockSpec(...  15.3 us
  transfers between devices with their start and end apart: 1, of which 0 were waited for; matrix products, arithmetic and copies ran while one was open for 0% of the time, Pallas kernels for 8%

profile of v3, /device:TPU:0, one launch (start us, length us, event | category | flops | bytes accessed | tf_op | source)
XLA Modules:
  0.0 200.8 jit_solution(1168528508475561648)
XLA Ops:
  0.0 2.8 %pad.4.legendre_ref = bf16[12,96,768]{2,1,0:T(8,128)(2,1)} pad(bf16[12,90,768]{2,1,0:T(8,128)(2,1)} %param.7, bf16[]{:T(256)} %constant.2.clone.1), padding=0_0x0_6x0_0 | pad | bytes 3428354 | tf_op jit(solution)/shard_map/jit(_pad)/pad | solution.py:478
  2.8 86.8 %fourier.1 = (bf16[12,8,96,384]{3,2,1,0:T(8,128)(2,1)}, bf16[8,8,96,768]{3,2,1,0:T(8,128)(2,1)}) custom-call(s32[48]{0:T(128)} %low_ref.3, bf16[3,180,32,1440]{3,2,1,0:T(8,128)(2,1)} %bitcast.2, bf16[12,96,768]{2,1,0:T(8,128)(2,1)} %pad.4.legendre_ref), custom_call_target="tpu_custom_call" | custom-call | tf_op jit(solution)/shard_map/fourier/pallas_call | solution.py:495
  89.7 75.2 %legendre.1 = (bf16[2,180,16,384]{3,2,1,0:T(8,128)(2,1)}, bf16[90,16,384]{2,1,0:T(8,128)(2,1)}, bf16[4,4,96,384]{3,2,1,0:T(8,128)(2,1)}, bf16[192,1440]{1,0:T(8,128)(2,1)}, bf16[4,8,96,768]{3,2,1,0:T(8,128)(2,1)}) custom-call(s32[48]{0:T(128)} %low_ref.3, bf16[12,8,96,384]{3,2,1,0:T(8,128)(2,1)} %get-tuple-element.11.coeffs_ref, ...), custom_call_target="tpu_custom_call" | custom-call | tf_op jit(solution)/shard_map/legendre/pallas_call | solution.py:520
  164.9 3.7 %all-to-all-start = ((bf16[4,4,96,384]{3,2,1,0:T(8,128)(2,1)}), bf16[4,4,96,384]{3,2,1,0:T(8,128)(2,1)S(1)}, u32[]{:S(2)}, u32[]{:S(2)}) async-start(bf16[4,4,96,384]{3,2,1,0:T(8,128)(2,1)} %get-tuple-element.14), calls=%async_computation | async-start | bytes 2359296 | tf_op jit(solution)/shard_map/all_to_all | solution.py:548
  168.6 15.3 %fourier_back.1._ = bf16[3,180,32,1440]{3,2,1,0:T(8,128)(2,1)} custom-call(f32[180]{0:T(256)} %weight_ref.3, bf16[2,180,16,384]{3,2,1,0:T(8,128)(2,1)} %get-tuple-element.13.band_ref, bf16[90,16,384]{2,1,0:T(8,128)(2,1)} %get-tuple-element.16.last_ref, bf16[192,1440]{1,0:T(8,128)(2,1)} %get-tuple-element.15.table_ref), custom_call_target="tpu_custom_call" | custom-call | flops 4777574400 | bytes 28200960 | tf_op jit(solution)/shard_map/fourier_back/pallas_call | solution.py:563
  183.9 0.0 all-to-all-done.rest_ref
  183.9 0.0 copy-start
  183.9 1.0 copy-done
  184.9 15.8 %fourier_back_rest.1 = bf16[3,180,32,1440]{3,2,1,0:T(8,128)(2,1)} custom-call(f32[180]{0:T(256)} %weight_ref.3, bf16[2,180,16,384]{3,2,1,0:T(8,128)(2,1)} %get-tuple-element.13.band_ref, bf16[4,4,96,384]{3,2,1,0:T(8,128)(2,1)} %copy-done, bf16[192,1440]{1,0:T(8,128)(2,1)} %get-tuple-element.15.table_ref, ...), custom_call_target="tpu_custom_call", output_to_operand_aliasing={{}: (4, {})} | custom-call | flops 4777574400 | bytes 28200960 | tf_op jit(solution)/shard_map/fourier_back_rest/pallas_call | solution.py:578
Async XLA Ops:
  164.9 19.0 %all-to-all-start = ((bf16[4,4,96,384]{3,2,1,0:T(8,128)(2,1)}), bf16[4,4,96,384]{3,2,1,0:T(8,128)(2,1)S(1)}, u32[]{:S(2)}, u32[]{:S(2)}) async-start(bf16[4,4,96,384]{3,2,1,0:T(8,128)(2,1)} %get-tuple-element.14), calls=%async_computation | async-start | bytes 2359296 | tf_op jit(solution)/shard_map/all_to_all | solution.py:548
  183.9 1.0 copy-start

commit v4 on v3

--- a/solution.py
+++ b/solution.py
@@ -183,19 +183,43 @@
     )
 
 
-def forward_kernel(
-    low_ref, x_ref, legendre_ref, out_ref, gathered_ref, x_buf, table_ref, turned_ref, stage_ref,
-    x_sem, send_sem, recv_sem, own_sem, up_sem, down_sem, flag_sem, *, devices, chips, groups, block_rows
+def spectral_kernel(
+    low_ref, x_ref, legendre_ref, filter_re_ref, filter_im_ref, *refs, devices, chips, groups, block_rows, sequence, sets
 ):
+    out_ref, last_ref, rest_ref, inverse_ref, coeffs_ref = refs[:5]
+    tables, refs = refs[5 : 5 + sets], refs[5 + sets :]
+    x_buf, table_ref, turned_ref, spent_ref, z_buf, l_buf, gains_ref, stage_ref, band_buf, wide_ref, rows_buf = refs[:11]
+    x_sem, there_sem, here_sem, kept_sem, z_sem, l_sem, send_sem, recv_sem, own_sem, out_sem, rest_sem = refs[11:22]
+    line_sems = refs[22:]
     samples, lat_local, channels, _ = x_ref.shape
-    pairs, blocks, padded, lanes = out_ref.shape
+    pairs, blocks, padded, lanes = coeffs_ref.shape
+    packed_rows = legendre_ref.shape[2]
     sc = samples * channels
+    half = lanes // 2
+    share = pairs // sets
+    full = pairs - share
     order = lax.axis_index("order")
     per_band = blocks // devices
     per_block = padded // TILE
     chunks = per_band * per_block
     slack = max(0, (per_band - 1) * block_rows + padded - lat_local)
-    line = Line(chips, 0, gathered_ref.shape[0], groups, legendre_ref, gathered_ref, (up_sem, down_sem, flag_sem))
+    rows = blocks * padded
+    band = rows // devices
+    head = band - padded
+    early_lat = lat_local - block_rows
+    count = devices * pairs
+    steps = (chips - 1) * groups
+    lines = [
+        Line(chips, p * share, share, groups, legendre_ref, tables[p], line_sems[3 * p : 3 * p + 3]) for p in range(sets)
+    ]
+
+    def advance(line, first, last):
+        def one(step, carry):
+            line.step(step // groups + 1, step % groups)
+            return carry
+
+        if last > first:
+            lax.fori_loop(first, last, one, 0)
 
     def x_copy(chunk):
         start = (chunk // per_block) * block_rows + (chunk % per_block) * TILE
@@ -207,12 +231,36 @@
 
     x_copy(0).start()
     enter(devices, chips)
-    line.start()
-    steps = (chips - 1) * groups
-    count = devices * pairs
+    for line in lines[:2]:
+        line.start()
     fill_forward(low_ref, table_ref, count)
 
-    def body(chunk, carry):
+    def give(chunk, first, size, part):
+        block = order * per_band + chunk // per_block
+        target = coeffs_ref.at[pl.ds(first, size), block, pl.ds((chunk % per_block) * TILE, TILE)]
+        for turn in range(1, devices):
+            peer = lax.rem(order + turn, devices)
+            src = spent_ref.at[chunk, pl.ds(peer * pairs + first, size)]
+            to_order(src, target, there_sem.at[turn, part], here_sem.at[turn, part], peer).start()
+        src = spent_ref.at[chunk, pl.ds(order * pairs + first, size)]
+        pltpu.make_async_copy(src, target, kept_sem.at[part]).start()
+
+    def take(first, size, part):
+        for turn in range(1, devices):
+            peer = lax.rem(order + turn, devices)
+            source = lax.rem(order + devices - turn, devices)
+            sent = coeffs_ref.at[pl.ds(first, size), pl.ds(peer * per_band, per_band)]
+            got = coeffs_ref.at[pl.ds(first, size), pl.ds(source * per_band, per_band)]
+            both = to_order(sent, got, there_sem.at[turn, part], here_sem.at[turn, part], peer)
+            both.wait_send()
+            both.wait_recv()
+        own = coeffs_ref.at[pl.ds(first, size), pl.ds(order * per_band, per_band)]
+        pltpu.make_async_copy(own, own, kept_sem.at[part]).wait()
+
+    first_step = chunks // 2 - 1
+    inner = min(steps, (chunks - first_step + 1) // 2)
+
+    def analyse(chunk, carry):
         slot = chunk % 2
         x_copy(chunk).wait()
 
@@ -225,170 +273,111 @@
         for t in range(TILE):
             turned = coeffs[t * sc : (t + 1) * sc].T
             turned_ref[t, :, 0:sc] = turned[: turned_ref.shape[1]]
-        block, part = chunk // per_block, chunk % per_block
-        live = lax.broadcasted_iota(jnp.int32, (TILE, lanes), 0) < block_rows - part * TILE
+        live = lax.broadcasted_iota(jnp.int32, (TILE, lanes), 0) < block_rows - (chunk % per_block) * TILE
         for pair in range(count):
             row = jnp.concatenate([turned_ref[:, q * count + pair, 0:sc] for q in range(4)], axis=1)
-            stage_ref[chunk, pair] = jnp.where(live, row, 0.0).astype(jnp.bfloat16)
-        target = out_ref.at[:, order * per_band + block, pl.ds(part * TILE, TILE)]
-        for turn in range(1, devices):
-            peer = lax.rem(order + turn, devices)
-            src = stage_ref.at[chunk, pl.ds(peer * pairs, pairs)]
-            to_order(src, target, send_sem.at[turn], recv_sem.at[turn], peer).start()
-        pltpu.make_async_copy(stage_ref.at[chunk, pl.ds(order * pairs, pairs)], target, own_sem).start()
-        step = chunk - 1
-
-        @pl.when((step >= 0) & (step < steps))
+            spent_ref[chunk, pair] = jnp.where(live, row, 0.0).astype(jnp.bfloat16)
+        give(chunk, 0, full, 0)
+        step = (chunk - first_step) // 2
+
+        @pl.when((chunk >= first_step) & ((chunk - first_step) % 2 == 0) & (step < inner))
         def _():
-            line.step(step // groups + 1, step % groups)
+            lines[0].step(step // groups + 1, step % groups)
 
         return carry
 
-    lax.fori_loop(0, chunks, body, 0)
-    if steps > chunks - 1:
-
-        def rest(step, carry):
-            line.step(step // groups + 1, step % groups)
-            return carry
-
-        lax.fori_loop(chunks - 1, steps, rest, 0)
-    for turn in range(1, devices):
-        peer = lax.rem(order + turn, devices)
-        source = lax.rem(order + devices - turn, devices)
-        sent = out_ref.at[:, pl.ds(peer * per_band, per_band)]
-        got = out_ref.at[:, pl.ds(source * per_band, per_band)]
-        both = to_order(sent, got, send_sem.at[turn], recv_sem.at[turn], peer)
-        both.wait_send()
-        both.wait_recv()
-    own = out_ref.at[:, pl.ds(order * per_band, per_band)]
-    pltpu.make_async_copy(own, own, own_sem).wait()
-    line.finish()
-
-
-def middle_kernel(
-    low_ref, coeffs_ref, early_ref, legendre_ref, filter_re_ref, filter_im_ref,
-    out_ref, last_ref, rest_ref, inverse_ref, late_ref, z_buf, l_buf, gains_ref, stage_ref, band_buf, wide_ref, rows_buf,
-    z_sem, l_sem, send_sem, recv_sem, own_sem, out_sem, rest_sem, up_sem, down_sem, flag_sem,
-    *, devices, chips, groups, samples, sequence
-):
-    pairs, blocks, padded, lanes = coeffs_ref.shape
-    packed_rows = legendre_ref.shape[2]
-    early = early_ref.shape[0]
-    rows = blocks * padded
-    band = rows // devices
-    half = lanes // 2
-    sc = half // 2
-    channels = sc // samples
-    order = lax.axis_index("order")
-    line = Line(chips, early, pairs - early, groups, legendre_ref, late_ref, (up_sem, down_sem, flag_sem))
-
-    def z_copy(pair):
-        return pltpu.make_async_copy(coeffs_ref.at[pair], z_buf.at[pair % 2], z_sem.at[pair % 2])
-
-    def l_copy(ref, entry, slot):
-        return pltpu.make_async_copy(ref.at[entry], l_buf.at[slot], l_sem.at[slot])
-
-    z_copy(0).start()
-    l_copy(early_ref, 0, 0).start()
-    enter(devices, chips)
-    line.start()
-    steps = (chips - 1) * groups
-    sets, share, lat_local = out_ref.shape[0] + 1, out_ref.shape[2] // devices, out_ref.shape[1]
-    head = band - padded
+    lax.fori_loop(0, chunks, analyse, 0)
+
+    def later(chunk, carry):
+        give(chunk, full, share, 1)
+        return carry
+
+    lax.fori_loop(0, chunks, later, 0)
     degrees = filter_re_ref.shape[1]
     filters = jnp.concatenate([filter_re_ref[...], filter_im_ref[...]], axis=0)
     filters = jnp.concatenate([filters, jnp.zeros((2 * channels, packed_rows - degrees), jnp.float32)], axis=1).T
     gains_ref[HEAD : HEAD + packed_rows] = filters
     gains_ref[HEAD + packed_rows :] = jnp.zeros((degrees, 2 * channels), jnp.float32)
     gains_ref[HEAD - 1 : HEAD] = filters[0:1]
+    fill_inverse(low_ref, inverse_ref, sequence)
     contract = (((0,), (0,)), ((), ()))
     row_ids = lax.broadcasted_iota(jnp.int32, (packed_rows, half), 0)
 
-    def body(pair, carry):
-        slot = pair % 2
-        z_copy(pair).wait()
-        l_copy(early_ref, 0, slot).wait()
-
-        @pl.when(pair + 1 < pairs)
-        def _():
-            z_copy(pair + 1).start()
-
-        @pl.when(pair + 1 < early)
-        def _():
-            l_copy(early_ref, pair + 1, 1 - slot).start()
-
-        @pl.when((pair + 1 >= early + 1) & (pair + 1 < pairs))
-        def _():
-            l_copy(late_ref, pair + 1 - early, 1 - slot).start()
-
-        legendre = l_buf[slot].reshape(rows, packed_rows)
-        coeffs = z_buf[slot].reshape(rows, lanes)
-        spectrum = lax.dot_general(legendre, coeffs, contract, preferred_element_type=jnp.float32)
-        low = low_ref[order * pairs + pair]
-        inside = row_ids < M - low
-        own = jnp.where(inside, spectrum[:, :half], spectrum[:, half:])
-        other = jnp.concatenate([own[:, sc:], own[:, :sc]], axis=1)
-        upper = gains_ref[pl.ds(low + HEAD, packed_rows), :]
-        gains = jnp.where(inside[:, : 2 * channels], upper, gains_ref[pl.ds(HEAD - 1, packed_rows), :])
-        gain_re = gains[:, :channels]
-        gain_im = gains[:, channels:]
-        gain_re = jnp.concatenate([gain_re] * (2 * samples), axis=1)
-        gain_im = jnp.concatenate([gain_im] * samples + [-gain_im] * samples, axis=1)
-        filtered = gain_re * own + gain_im * other
-        zeros = jnp.zeros_like(filtered)
-        split = jnp.concatenate([jnp.where(inside, filtered, zeros), jnp.where(inside, zeros, filtered)], axis=1)
-        synthesis = jnp.dot(legendre, split.astype(jnp.bfloat16), preferred_element_type=jnp.float32)
-        stage_ref[pair] = synthesis.astype(jnp.bfloat16)
-        bundle = pair // share
-
-        def send(size, part):
-            target = band_buf.at[bundle, order, pair % share, pl.ds(0, size)]
-            for turn in range(1, devices):
-                peer = lax.rem(order + turn, devices)
-                src = stage_ref.at[pair, pl.ds(peer * band, size)]
-                to_order(src, target, send_sem.at[turn, part], recv_sem.at[turn, bundle], peer).start()
-            src = stage_ref.at[pair, pl.ds(order * band, size)]
-            pltpu.make_async_copy(src, target, own_sem.at[bundle]).start()
-
-        @pl.when(bundle < sets - 1)
-        def _():
-            send(band, 0)
-
-        @pl.when(bundle == sets - 1)
-        def _():
-            send(head, 1)
-            for device in range(devices):
-                src = stage_ref.at[pair, pl.ds(device * band + head, padded)]
-                pltpu.make_async_copy(src, rest_ref.at[device, pair % share], rest_sem).start()
-
-        @pl.when(pair + 1 == early)
-        def _():
-            def gather(step, carry):
-                line.step(step // groups + 1, step % groups)
-                return carry
-
-            lax.fori_loop((early - 1) // 2, steps, gather, 0)
-            line.finish()
-            l_copy(late_ref, 0, 1 - slot).start()
-
-        @pl.when((pair + 1 < early) & (pair % 2 == 1) & (pair // 2 < steps))
-        def _():
-            step = pair // 2
-            line.step(step // groups + 1, step % groups)
-
-        return carry
-
-    lax.fori_loop(0, pairs, body, 0)
-    fill_inverse(low_ref, inverse_ref, sequence)
-    block_rows = lat_local // (blocks // devices)
-    early_lat = lat_local - block_rows
+    def z_copy(pair):
+        return pltpu.make_async_copy(coeffs_ref.at[pair], z_buf.at[pair % 2], z_sem.at[pair % 2])
+
+    def send(pair, bundle, size, part):
+        target = band_buf.at[bundle, order, pair % share, pl.ds(0, size)]
+        for turn in range(1, devices):
+            peer = lax.rem(order + turn, devices)
+            src = stage_ref.at[pair, pl.ds(peer * band, size)]
+            to_order(src, target, send_sem.at[turn, part], recv_sem.at[turn, bundle], peer).start()
+        src = stage_ref.at[pair, pl.ds(order * band, size)]
+        pltpu.make_async_copy(src, target, own_sem.at[bundle]).start()
+
+    def middle(bundle, ahead, first_step):
+        base = bundle * share
+        table = tables[bundle]
+
+        def l_copy(pair):
+            return pltpu.make_async_copy(table.at[pair - base], l_buf.at[pair % 2], l_sem.at[pair % 2])
+
+        z_copy(base).start()
+        l_copy(base).start()
+
+        def one(pair, carry):
+            slot = pair % 2
+            z_copy(pair).wait()
+            l_copy(pair).wait()
+
+            @pl.when(pair + 1 < base + share)
+            def _():
+                z_copy(pair + 1).start()
+                l_copy(pair + 1).start()
+
+            legendre = l_buf[slot].reshape(rows, packed_rows)
+            coeffs = z_buf[slot].reshape(rows, lanes)
+            spectrum = lax.dot_general(legendre, coeffs, contract, preferred_element_type=jnp.float32)
+            low = low_ref[order * pairs + pair]
+            inside = row_ids < M - low
+            own = jnp.where(inside, spectrum[:, :half], spectrum[:, half:])
+            other = jnp.concatenate([own[:, sc:], own[:, :sc]], axis=1)
+            upper = gains_ref[pl.ds(low + HEAD, packed_rows), :]
+            gains = jnp.where(inside[:, : 2 * channels], upper, gains_ref[pl.ds(HEAD - 1, packed_rows), :])
+            gain_re = gains[:, :channels]
+            gain_im = gains[:, channels:]
+            gain_re = jnp.concatenate([gain_re] * (2 * samples), axis=1)
+            gain_im = jnp.concatenate([gain_im] * samples + [-gain_im] * samples, axis=1)
+            filtered = gain_re * own + gain_im * other
+            zeros = jnp.zeros_like(filtered)
+            split = jnp.concatenate([jnp.where(inside, filtered, zeros), jnp.where(inside, zeros, filtered)], axis=1)
+            synthesis = jnp.dot(legendre, split.astype(jnp.bfloat16), preferred_element_type=jnp.float32)
+            stage_ref[pair] = synthesis.astype(jnp.bfloat16)
+            if bundle < sets - 1:
+                send(pair, bundle, band, 0)
+            else:
+                send(pair, bundle, head, 1)
+                for device in range(devices):
+                    src = stage_ref.at[pair, pl.ds(device * band + head, padded)]
+                    pltpu.make_async_copy(src, rest_ref.at[device, pair % share], rest_sem).start()
+            if ahead is not None:
+                step = first_step + (pair - base) // 2
+
+                @pl.when(((pair - base) % 2 == 1) & (step < steps))
+                def _():
+                    ahead.step(step // groups + 1, step % groups)
+
+            return carry
+
+        lax.fori_loop(base, base + share, one, 0)
 
     def rows_copy(bundle):
-        if bundle is None:
-            return pltpu.make_async_copy(rows_buf.at[sets - 1, pl.ds(0, early_lat)], last_ref, out_sem.at[sets - 1])
-        return pltpu.make_async_copy(rows_buf.at[bundle], out_ref.at[bundle], out_sem.at[bundle])
-
-    def spread(bundle, size, lats):
+        if bundle == sets - 1:
+            return pltpu.make_async_copy(rows_buf.at[pl.ds(0, early_lat)], last_ref, out_sem.at[bundle])
+        return pltpu.make_async_copy(rows_buf, out_ref.at[bundle], out_sem.at[bundle])
+
+    def spread(bundle):
+        size, lats = (band, lat_local) if bundle < sets - 1 else (head, early_lat)
         for turn in range(1, devices):
             source = lax.rem(order + devices - turn, devices)
             got = band_buf.at[bundle, source, :, pl.ds(0, size)]
@@ -398,23 +387,44 @@
         for device in range(devices):
             for entry in range(share):
                 wide_ref[device * share + entry, 0:size] = band_buf[bundle, device, entry, 0:size].astype(jnp.float32)
+        if bundle > 0:
+            rows_copy(bundle - 1).wait()
 
         def turn_row(lat, carry):
             row = (lat // block_rows) * padded + lat % block_rows
-            rows_buf[bundle, lat] = wide_ref[:, row].astype(jnp.bfloat16)
+            rows_buf[lat] = wide_ref[:, row].astype(jnp.bfloat16)
             return carry
 
         lax.fori_loop(0, lats, turn_row, 0, unroll=step_of(lats, 10))
-
-    def whole(bundle, carry):
-        spread(bundle, band, lat_local)
         rows_copy(bundle).start()
-        return carry
-
-    lax.fori_loop(0, sets - 1, whole, 0)
-    spread(sets - 1, head, early_lat)
-    rows_copy(None).start()
-    full = pairs - share
+
+    advance(lines[0], inner, steps)
+    lines[0].finish()
+    done = min(groups, steps)
+    advance(lines[1], 0, done)
+    take(0, full, 0)
+    for bundle in range(sets):
+        if bundle == sets - 1:
+            take(full, share, 1)
+        ahead = lines[bundle + 1] if bundle + 1 < sets else None
+        if bundle == 0:
+            middle(bundle, ahead, done)
+            done = min(steps, done + share // 2)
+        else:
+            middle(bundle, None, 0)
+            done = 0
+        if bundle + 2 < sets:
+            lines[bundle + 2].start()
+        if ahead is not None:
+            if bundle > 0:
+                advance(ahead, done, steps - groups)
+                done = max(done, steps - groups)
+                spread(bundle - 1)
+            advance(ahead, done, steps)
+            ahead.finish()
+        elif bundle > 0:
+            spread(bundle - 1)
+    spread(sets - 1)
     for turn in range(1, devices):
         peer = lax.rem(order + turn, devices)
         sent = stage_ref.at[pl.ds(0, full), pl.ds(peer * band, band)]
@@ -422,9 +432,7 @@
         sent = stage_ref.at[pl.ds(full, share), pl.ds(peer * band, head)]
         to_order(sent, sent, send_sem.at[turn, 1], recv_sem.at[turn, 0], peer).wait_send()
     pltpu.make_async_copy(rest_ref, rest_ref, rest_sem).wait()
-    for bundle in range(sets - 1):
-        rows_copy(bundle).wait()
-    rows_copy(None).wait()
+    rows_copy(sets - 1).wait()
 
 
 def emit(row_sets, start, weight_ref, table_ref, out_ref):
@@ -472,9 +480,9 @@
     per_band = lat_local // block_rows
     chips = members // 2
     columns = devices * pairs * 4
-    early = (2 * pairs) // 3
-    early_groups = step_of(early, 4)
-    late_groups = step_of(pairs - early, 2)
+    share = step_of(pairs, 4)
+    sets = pairs // share
+    groups = step_of(share, 2)
     legendre = jnp.pad(legendre, ((0, 0), (0, padded - block_rows), (0, 0)))
     hbm = pl.BlockSpec(memory_space=pl.ANY)
     vmem = pl.BlockSpec(memory_space=pltpu.VMEM)
@@ -484,66 +492,46 @@
     chunks = per_band * padded // TILE
     slack = max(0, (per_band - 1) * block_rows + padded - lat_local)
 
-    def params(collective_id):
-        return pltpu.CompilerParams(
-            collective_id=collective_id, has_side_effects=True, vmem_limit_bytes=60 << 20
-        )
-
-    def line_sems(groups):
-        return [dma((chips, groups)), dma((chips, groups)), dma((5,))]
-
-    coeffs, early_table = pl.pallas_call(
+    sequence = [d * pairs + g * share + j for g in range(sets) for d in range(devices) for j in range(share)]
+    rows = per_band * padded
+    line = [dma((chips, groups)), dma((chips, groups)), dma((5,))]
+    outs = pl.pallas_call(
         functools.partial(
-            forward_kernel, devices=devices, chips=chips, groups=early_groups, block_rows=block_rows
+            spectral_kernel, devices=devices, chips=chips, groups=groups, block_rows=block_rows,
+            sequence=sequence, sets=sets
         ),
-        in_specs=[smem, hbm, vmem],
-        out_specs=[hbm, hbm],
+        in_specs=[smem, hbm, vmem, vmem, vmem],
+        out_specs=[hbm, hbm, hbm, vmem, hbm] + [hbm] * sets,
         out_shape=[
+            jax.ShapeDtypeStruct((sets - 1, lat_local, devices * share, lanes), bf16),
+            jax.ShapeDtypeStruct((lat_local - block_rows, devices * share, lanes), bf16),
+            jax.ShapeDtypeStruct((devices, share, padded, lanes), bf16),
+            jax.ShapeDtypeStruct((columns, longitudes), bf16),
             jax.ShapeDtypeStruct((pairs, members, padded, lanes), bf16),
-            jax.ShapeDtypeStruct((early, members, padded, packed_rows), bf16),
-        ],
+        ]
+        + [jax.ShapeDtypeStruct((share, members, padded, packed_rows), bf16)] * sets,
         scratch_shapes=[
             pltpu.VMEM((2, samples, TILE + slack, channels, longitudes), bf16),
             pltpu.VMEM((longitudes, -(-columns // 128) * 128), bf16),
             pltpu.VMEM((TILE, columns, -(-(samples * channels) // 128) * 128), jnp.float32),
             pltpu.VMEM((chunks, devices * pairs, TILE, lanes), bf16),
-            dma((2,)), dma((devices,)), dma((devices,)), dma, *line_sems(early_groups),
-        ],
-        compiler_params=params(0),
-        name="fourier",
-    )(pair_order, jnp.transpose(grad_out, (0, 2, 1, 3)), legendre)
-
-    share = step_of(pairs, 4)
-    sets = pairs // share
-    sequence = [d * pairs + g * share + j for g in range(sets) for d in range(devices) for j in range(share)]
-    rows = per_band * padded
-    band, last, rest, inverse, _ = pl.pallas_call(
-        functools.partial(
-            middle_kernel, devices=devices, chips=chips, groups=late_groups, samples=samples, sequence=sequence
-        ),
-        in_specs=[smem, hbm, hbm, vmem, vmem, vmem],
-        out_specs=[hbm, hbm, hbm, vmem, hbm],
-        out_shape=[
-            jax.ShapeDtypeStruct((sets - 1, lat_local, devices * share, lanes), bf16),
-            jax.ShapeDtypeStruct((lat_local - block_rows, devices * share, lanes), bf16),
-            jax.ShapeDtypeStruct((devices, share, padded, lanes), bf16),
-            jax.ShapeDtypeStruct((columns, longitudes), bf16),
-            jax.ShapeDtypeStruct((pairs - early, members, padded, packed_rows), bf16),
-        ],
-        scratch_shapes=[
             pltpu.VMEM((2, members, padded, lanes), bf16),
             pltpu.VMEM((2, members, padded, packed_rows), bf16),
             pltpu.VMEM((HEAD + packed_rows + filter_re.shape[1], 2 * channels), jnp.float32),
             pltpu.VMEM((pairs, members * padded, lanes), bf16),
             pltpu.VMEM((sets, devices, share, rows, lanes), bf16),
             pltpu.VMEM((devices * share, rows, lanes), jnp.float32),
-            pltpu.VMEM((sets, lat_local, devices * share, lanes), bf16),
-            dma((2,)), dma((2,)), dma((devices, 2)), dma((devices, sets)), dma((sets,)), dma((sets,)), dma,
-            *line_sems(late_groups),
+            pltpu.VMEM((lat_local, devices * share, lanes), bf16),
+            dma((2,)), dma((devices, 2)), dma((devices, 2)), dma((2,)), dma((2,)), dma((2,)),
+            dma((devices, 2)), dma((devices, sets)), dma((sets,)), dma((sets,)), dma,
+            *(line * sets),
         ],
-        compiler_params=params(1),
-        name="legendre",
-    )(pair_order, coeffs, early_table, legendre, filter_re, filter_im)
+        compiler_params=pltpu.CompilerParams(
+            collective_id=0, has_side_effects=True, vmem_limit_bytes=67043328
+        ),
+        name="spectral",
+    )(pair_order, jnp.transpose(grad_out, (0, 2, 1, 3)), legendre, filter_re, filter_im)
+    band, last, rest, inverse = outs[:4]
 
     rest = lax.all_to_all(rest, "order", split_axis=0, concat_axis=0, tiled=True)
     steps = step_of(block_rows, 18)

time: 201 us -> 194 us (0.965)
  Pallas kernels: 193 us -> 186 us
    pallas_call x2 -> x1, Pallas kernels: 162 us -> 155 us  [body(): pl.pallas_call(functools.partial(spectral_kernel, devices=devices, chips=...]
where the time goes in v4:
time: 194 us
  Pallas kernels  186 us (96%)
  local copies, waits for them, and re-layouts  3.88 us (2%)
  starting transfers between devices  3.72 us (2%)
    pallas_call x1, Pallas kernels, body(): pl.pallas_call(functools.partial(spectral_kernel, devices=devices, chips=...  155 us
    pallas_call x1, Pallas kernels, body(): pl.pallas_call(functools.partial(second_kernel, offset=early_lat), grid=(...  15.9 us
    pallas_call x1, Pallas kernels, body(): pl.pallas_call(first_kernel, grid=(ahead,), in_specs=[smem, pl.BlockSpec(...  15.3 us
  transfers between devices with their start and end apart: 1, of which 0 were waited for; matrix products, arithmetic and copies ran while one was open for 0% of the time, Pallas kernels for 8%

profile of v4, /device:TPU:0, one launch (start us, length us, event | category | flops | bytes accessed | tf_op | source)
XLA Modules:
  0.0 193.6 jit_solution(13888062884139685909)
XLA Ops:
  0.0 2.8 %pad.4.legendre_ref = bf16[12,96,768]{2,1,0:T(8,128)(2,1)} pad(bf16[12,90,768]{2,1,0:T(8,128)(2,1)} %param.7, bf16[]{:T(256)} %constant.2.clone.1), padding=0_0x0_6x0_0 | pad | bytes 3428354 | tf_op jit(solution)/shard_map/jit(_pad)/pad | solution.py:486
  2.8 154.9 %spectral.1 = (bf16[2,180,16,384]{3,2,1,0:T(8,128)(2,1)}, bf16[90,16,384]{2,1,0:T(8,128)(2,1)}, bf16[4,4,96,384]{3,2,1,0:T(8,128)(2,1)}, bf16[192,1440]{1,0:T(8,...) custom-call(s32[48]{0:T(128)} %low_ref.1, ...), custom_call_target="tpu_custom_call" | custom-call | tf_op jit(solution)/shard_map/spectral/pallas_call | solution.py:498
  157.7 3.7 %all-to-all-start = ((bf16[4,4,96,384]{3,2,1,0:T(8,128)(2,1)}), bf16[4,4,96,384]{3,2,1,0:T(8,128)(2,1)S(1)}, u32[]{:S(2)}, u32[]{:S(2)}) async-start(bf16[4,4,96,384]{3,2,1,0:T(8,128)(2,1)} %get-tuple-element.10), calls=%async_computation | async-start | bytes 2359296 | tf_op jit(solution)/shard_map/all_to_all | solution.py:536
  161.4 15.3 %fourier_back.1._ = bf16[3,180,32,1440]{3,2,1,0:T(8,128)(2,1)} custom-call(f32[180]{0:T(256)} %weight_ref.3, bf16[2,180,16,384]{3,2,1,0:T(8,128)(2,1)} %get-tuple-element.9.band_ref, bf16[90,16,384]{2,1,0:T(8,128)(2,1)} %get-tuple-element.12.last_ref, bf16[192,1440]{1,0:T(8,128)(2,1)} %get-tuple-element.11.table_ref), custom_call_target="tpu_custom_call" | custom-call | flops 4777574400 | bytes 28200960 | tf_op jit(solution)/shard_map/fourier_back/pallas_call | solution.py:551
  176.7 0.0 all-to-all-done.rest_ref
  176.7 0.0 copy-start
  176.7 1.0 copy-done
  177.8 15.9 %fourier_back_rest.1 = bf16[3,180,32,1440]{3,2,1,0:T(8,128)(2,1)} custom-call(f32[180]{0:T(256)} %weight_ref.3, bf16[2,180,16,384]{3,2,1,0:T(8,128)(2,1)} %get-tuple-element.9.band_ref, bf16[4,4,96,384]{3,2,1,0:T(8,128)(2,1)} %copy-done, bf16[192,1440]{1,0:T(8,128)(2,1)} %get-tuple-element.11.table_ref, ...), custom_call_target="tpu_custom_call", output_to_operand_aliasing={{}: (4, {})} | custom-call | flops 4777574400 | bytes 28200960 | tf_op jit(solution)/shard_map/fourier_back_rest/pallas_call | solution.py:566
Async XLA Ops:
  157.7 19.0 %all-to-all-start = ((bf16[4,4,96,384]{3,2,1,0:T(8,128)(2,1)}), bf16[4,4,96,384]{3,2,1,0:T(8,128)(2,1)S(1)}, u32[]{:S(2)}, u32[]{:S(2)}) async-start(bf16[4,4,96,384]{3,2,1,0:T(8,128)(2,1)} %get-tuple-element.10), calls=%async_computation | async-start | bytes 2359296 | tf_op jit(solution)/shard_map/all_to_all | solution.py:536
  176.7 1.0 copy-start

commit v5 on v4

--- a/solution.py
+++ b/solution.py
@@ -13,6 +13,7 @@
 TILE = 16
 FINE = 32
 HEAD = 8
+ALIGN = 8
 MESH = pl.DeviceIdType.MESH
 
 
@@ -184,18 +185,21 @@
 
 
 def spectral_kernel(
-    low_ref, x_ref, legendre_ref, filter_re_ref, filter_im_ref, *refs, devices, chips, groups, block_rows, sequence, sets
+    low_ref, x_ref, block_ref, filter_re_ref, filter_im_ref, *refs, devices, chips, groups, block_rows, sequence, sets
 ):
     out_ref, last_ref, rest_ref, inverse_ref, coeffs_ref = refs[:5]
     tables, refs = refs[5 : 5 + sets], refs[5 + sets :]
+    legendre_ref, end_ref, ends_ref, end_buf, refs = *refs[:4], refs[4:]
     x_buf, table_ref, turned_ref, spent_ref, z_buf, l_buf, gains_ref, stage_ref, band_buf, wide_ref, rows_buf = refs[:11]
     x_sem, there_sem, here_sem, kept_sem, z_sem, l_sem, send_sem, recv_sem, own_sem, out_sem, rest_sem = refs[11:22]
     line_sems = refs[22:]
     samples, lat_local, channels, _ = x_ref.shape
-    pairs, blocks, padded, lanes = coeffs_ref.shape
-    packed_rows = legendre_ref.shape[2]
+    pairs, _, packed, lanes = coeffs_ref.shape
+    _, blocks, padded, packed_rows = l_buf.shape
     sc = samples * channels
     half = lanes // 2
+    main, ends = padded - ALIGN, end_ref.shape[2]
+    tail = block_rows - main
     share = pairs // sets
     full = pairs - share
     order = lax.axis_index("order")
@@ -231,30 +235,49 @@
 
     x_copy(0).start()
     enter(devices, chips)
+    for pair in range(pairs):
+        legendre_ref[pair, 0:main] = block_ref[pair, 0:main]
+        rows_left = block_ref[pair, main:block_rows].astype(jnp.float32)
+        rows_left = jnp.concatenate([rows_left, jnp.zeros((padded - block_rows, packed_rows), jnp.float32)], axis=0)
+        legendre_ref[pair, main:padded] = rows_left.astype(jnp.bfloat16)
     for line in lines[:2]:
         line.start()
     fill_forward(low_ref, table_ref, count)
 
-    def give(chunk, first, size, part):
-        block = order * per_band + chunk // per_block
-        target = coeffs_ref.at[pl.ds(first, size), block, pl.ds((chunk % per_block) * TILE, TILE)]
+    def give_rows(source_ref, entry, place, size, first, number, part):
+        target = coeffs_ref.at[pl.ds(first, number), order, pl.ds(place, size)]
         for turn in range(1, devices):
             peer = lax.rem(order + turn, devices)
-            src = spent_ref.at[chunk, pl.ds(peer * pairs + first, size)]
+            src = source_ref.at[entry, pl.ds(peer * pairs + first, number), pl.ds(0, size)]
             to_order(src, target, there_sem.at[turn, part], here_sem.at[turn, part], peer).start()
-        src = spent_ref.at[chunk, pl.ds(order * pairs + first, size)]
+        src = source_ref.at[entry, pl.ds(order * pairs + first, number), pl.ds(0, size)]
         pltpu.make_async_copy(src, target, kept_sem.at[part]).start()
 
-    def take(first, size, part):
+    def give(chunk, first, number, part):
+        within = chunk % per_block
+        place = (chunk // per_block) * main + within * TILE
+
+        @pl.when(within < per_block - 1)
+        def _():
+            give_rows(spent_ref, chunk, place, TILE, first, number, part)
+
+        @pl.when(within == per_block - 1)
+        def _():
+            give_rows(spent_ref, chunk, place, main - (per_block - 1) * TILE, first, number, part)
+
+    def give_ends(first, number, part):
+        give_rows(end_ref, 0, per_band * main, ends, first, number, part)
+
+    def take(first, number, part):
         for turn in range(1, devices):
             peer = lax.rem(order + turn, devices)
             source = lax.rem(order + devices - turn, devices)
-            sent = coeffs_ref.at[pl.ds(first, size), pl.ds(peer * per_band, per_band)]
-            got = coeffs_ref.at[pl.ds(first, size), pl.ds(source * per_band, per_band)]
+            sent = coeffs_ref.at[pl.ds(first, number), peer]
+            got = coeffs_ref.at[pl.ds(first, number), source]
             both = to_order(sent, got, there_sem.at[turn, part], here_sem.at[turn, part], peer)
             both.wait_send()
             both.wait_recv()
-        own = coeffs_ref.at[pl.ds(first, size), pl.ds(order * per_band, per_band)]
+        own = coeffs_ref.at[pl.ds(first, number), order]
         pltpu.make_async_copy(own, own, kept_sem.at[part]).wait()
 
     first_step = chunks // 2 - 1
@@ -288,6 +311,20 @@
 
     lax.fori_loop(0, chunks, analyse, 0)
 
+    def collect(pair, carry):
+        last = main - (per_block - 1) * TILE
+        pieces = []
+        for block in range(per_band):
+            rows_left = spent_ref[block * per_block + per_block - 1, pair].astype(jnp.float32)
+            pieces.append(rows_left[last : last + tail])
+        pieces.append(jnp.zeros((ends - per_band * tail, lanes), jnp.float32))
+        end_ref[0, pair] = jnp.concatenate(pieces, axis=0).astype(jnp.bfloat16)
+        return carry
+
+    lax.fori_loop(0, count, collect, 0)
+    give_ends(0, full, 0)
+    give_ends(full, share, 1)
+
     def later(chunk, carry):
         give(chunk, full, share, 1)
         return carry
@@ -303,17 +340,47 @@
     contract = (((0,), (0,)), ((), ()))
     row_ids = lax.broadcasted_iota(jnp.int32, (packed_rows, half), 0)
 
+    class Loads:
+        def __init__(self, pair):
+            slot = pair % 2
+            source = coeffs_ref.at[pair]
+            self.copies = [
+                pltpu.make_async_copy(
+                    source.at[:, pl.ds(block * main, main)], z_buf.at[slot, :, block, pl.ds(0, main)], z_sem.at[slot, block]
+                )
+                for block in range(per_band)
+            ]
+            last = source.at[:, pl.ds(per_band * main, ends)]
+            self.copies.append(pltpu.make_async_copy(last, end_buf.at[slot], z_sem.at[slot, per_band]))
+
+        def start(self):
+            for copy in self.copies:
+                copy.start()
+
+        def wait(self):
+            for copy in self.copies:
+                copy.wait()
+
     def z_copy(pair):
-        return pltpu.make_async_copy(coeffs_ref.at[pair], z_buf.at[pair % 2], z_sem.at[pair % 2])
-
-    def send(pair, bundle, size, part):
-        target = band_buf.at[bundle, order, pair % share, pl.ds(0, size)]
+        return Loads(pair)
+
+    def pass_on(src_of, target, bundle, part):
         for turn in range(1, devices):
             peer = lax.rem(order + turn, devices)
-            src = stage_ref.at[pair, pl.ds(peer * band, size)]
-            to_order(src, target, send_sem.at[turn, part], recv_sem.at[turn, bundle], peer).start()
-        src = stage_ref.at[pair, pl.ds(order * band, size)]
-        pltpu.make_async_copy(src, target, own_sem.at[bundle]).start()
+            to_order(src_of(peer), target, send_sem.at[turn, part], recv_sem.at[turn, bundle], peer).start()
+        pltpu.make_async_copy(src_of(order), target, own_sem.at[bundle]).start()
+
+    def send(pair, bundle):
+        target = band_buf.at[bundle, order, pair % share]
+        if bundle == sets - 1:
+            pass_on(lambda d: stage_ref.at[pair, pl.ds(d * band, head)], target.at[pl.ds(0, head)], bundle, 1)
+            return
+        for block in range(per_band):
+            pass_on(
+                lambda d: stage_ref.at[pair, pl.ds(d * band + block * padded, main)],
+                target.at[pl.ds(block * main, main)], bundle, 0,
+            )
+        pass_on(lambda d: ends_ref.at[pair, d], target.at[pl.ds(per_band * main, ends)], bundle, 0)
 
     def middle(bundle, ahead, first_step):
         base = bundle * share
@@ -336,6 +403,12 @@
                 l_copy(pair + 1).start()
 
             legendre = l_buf[slot].reshape(rows, packed_rows)
+            for device in range(devices):
+                rows_left = end_buf[slot, device].astype(jnp.float32)
+                for block in range(per_band):
+                    piece = rows_left[block * tail : (block + 1) * tail]
+                    piece = jnp.concatenate([piece, jnp.zeros((ALIGN - tail, lanes), jnp.float32)], axis=0)
+                    z_buf[slot, device, block, main:padded] = piece.astype(jnp.bfloat16)
             coeffs = z_buf[slot].reshape(rows, lanes)
             spectrum = lax.dot_general(legendre, coeffs, contract, preferred_element_type=jnp.float32)
             low = low_ref[order * pairs + pair]
@@ -354,9 +427,13 @@
             synthesis = jnp.dot(legendre, split.astype(jnp.bfloat16), preferred_element_type=jnp.float32)
             stage_ref[pair] = synthesis.astype(jnp.bfloat16)
             if bundle < sets - 1:
-                send(pair, bundle, band, 0)
-            else:
-                send(pair, bundle, head, 1)
+                for device in range(devices):
+                    starts = [device * band + block * padded + main for block in range(per_band)]
+                    pieces = [synthesis[start : start + tail] for start in starts]
+                    pieces.append(jnp.zeros((ends - per_band * tail, lanes), jnp.float32))
+                    ends_ref[pair, device] = jnp.concatenate(pieces, axis=0).astype(jnp.bfloat16)
+            send(pair, bundle)
+            if bundle == sets - 1:
                 for device in range(devices):
                     src = stage_ref.at[pair, pl.ds(device * band + head, padded)]
                     pltpu.make_async_copy(src, rest_ref.at[device, pair % share], rest_sem).start()
@@ -377,7 +454,7 @@
         return pltpu.make_async_copy(rows_buf, out_ref.at[bundle], out_sem.at[bundle])
 
     def spread(bundle):
-        size, lats = (band, lat_local) if bundle < sets - 1 else (head, early_lat)
+        size, lats = (packed, lat_local) if bundle < sets - 1 else (head, early_lat)
         for turn in range(1, devices):
             source = lax.rem(order + devices - turn, devices)
             got = band_buf.at[bundle, source, :, pl.ds(0, size)]
@@ -391,7 +468,13 @@
             rows_copy(bundle - 1).wait()
 
         def turn_row(lat, carry):
-            row = (lat // block_rows) * padded + lat % block_rows
+            block, within = lat // block_rows, lat % block_rows
+            if bundle < sets - 1:
+                over = jnp.maximum(within - main + 1, 0)
+                past = jnp.minimum(over, 1)
+                row = (1 - past) * (block * main + within) + past * (per_band * main + block * tail + over - 1)
+            else:
+                row = block * padded + within
             rows_buf[lat] = wide_ref[:, row].astype(jnp.bfloat16)
             return carry
 
@@ -427,9 +510,9 @@
     spread(sets - 1)
     for turn in range(1, devices):
         peer = lax.rem(order + turn, devices)
-        sent = stage_ref.at[pl.ds(0, full), pl.ds(peer * band, band)]
+        sent = band_buf.at[pl.ds(0, sets - 1), peer]
         to_order(sent, sent, send_sem.at[turn, 0], recv_sem.at[turn, 0], peer).wait_send()
-        sent = stage_ref.at[pl.ds(full, share), pl.ds(peer * band, head)]
+        sent = band_buf.at[sets - 1, peer, :, pl.ds(0, head)]
         to_order(sent, sent, send_sem.at[turn, 1], recv_sem.at[turn, 0], peer).wait_send()
     pltpu.make_async_copy(rest_ref, rest_ref, rest_sem).wait()
     rows_copy(sets - 1).wait()
@@ -456,12 +539,15 @@
     emit(row_sets, pl.program_id(0) * out_ref.shape[1], weight_ref, table_ref, out_ref)
 
 
-def second_kernel(weight_ref, band_ref, rest_ref, table_ref, _, out_ref, wide_ref, *, offset):
+def second_kernel(weight_ref, band_ref, source_ref, table_ref, _, out_ref, rest_ref, wide_ref, sem, *, offset):
     steps = out_ref.shape[1]
     part = pl.program_id(0)
 
     @pl.when(part == 0)
     def _():
+        copy = pltpu.make_async_copy(source_ref, rest_ref, sem)
+        copy.start()
+        copy.wait()
         devices, share, _, _ = rest_ref.shape
         for device in range(devices):
             for entry in range(share):
@@ -483,7 +569,9 @@
     share = step_of(pairs, 4)
     sets = pairs // share
     groups = step_of(share, 2)
-    legendre = jnp.pad(legendre, ((0, 0), (0, padded - block_rows), (0, 0)))
+    main = padded - ALIGN
+    ends = -(-per_band * (block_rows - main) // ALIGN) * ALIGN
+    packed = per_band * main + ends
     hbm = pl.BlockSpec(memory_space=pl.ANY)
     vmem = pl.BlockSpec(memory_space=pltpu.VMEM)
     smem = pl.BlockSpec(memory_space=pltpu.SMEM)
@@ -493,7 +581,6 @@
     slack = max(0, (per_band - 1) * block_rows + padded - lat_local)
 
     sequence = [d * pairs + g * share + j for g in range(sets) for d in range(devices) for j in range(share)]
-    rows = per_band * padded
     line = [dma((chips, groups)), dma((chips, groups)), dma((5,))]
     outs = pl.pallas_call(
         functools.partial(
@@ -507,22 +594,26 @@
             jax.ShapeDtypeStruct((lat_local - block_rows, devices * share, lanes), bf16),
             jax.ShapeDtypeStruct((devices, share, padded, lanes), bf16),
             jax.ShapeDtypeStruct((columns, longitudes), bf16),
-            jax.ShapeDtypeStruct((pairs, members, padded, lanes), bf16),
+            jax.ShapeDtypeStruct((pairs, devices, packed, lanes), bf16),
         ]
         + [jax.ShapeDtypeStruct((share, members, padded, packed_rows), bf16)] * sets,
         scratch_shapes=[
+            pltpu.VMEM((pairs, padded, packed_rows), bf16),
+            pltpu.VMEM((1, devices * pairs, ends, lanes), bf16),
+            pltpu.VMEM((pairs, devices, ends, lanes), bf16),
+            pltpu.VMEM((2, devices, ends, lanes), bf16),
             pltpu.VMEM((2, samples, TILE + slack, channels, longitudes), bf16),
             pltpu.VMEM((longitudes, -(-columns // 128) * 128), bf16),
             pltpu.VMEM((TILE, columns, -(-(samples * channels) // 128) * 128), jnp.float32),
             pltpu.VMEM((chunks, devices * pairs, TILE, lanes), bf16),
-            pltpu.VMEM((2, members, padded, lanes), bf16),
+            pltpu.VMEM((2, devices, per_band, padded, lanes), bf16),
             pltpu.VMEM((2, members, padded, packed_rows), bf16),
             pltpu.VMEM((HEAD + packed_rows + filter_re.shape[1], 2 * channels), jnp.float32),
             pltpu.VMEM((pairs, members * padded, lanes), bf16),
-            pltpu.VMEM((sets, devices, share, rows, lanes), bf16),
-            pltpu.VMEM((devices * share, rows, lanes), jnp.float32),
+            pltpu.VMEM((sets, devices, share, packed, lanes), bf16),
+            pltpu.VMEM((devices * share, packed, lanes), jnp.float32),
             pltpu.VMEM((lat_local, devices * share, lanes), bf16),
-            dma((2,)), dma((devices, 2)), dma((devices, 2)), dma((2,)), dma((2,)), dma((2,)),
+            dma((2,)), dma((devices, 2)), dma((devices, 2)), dma((2,)), dma((2, per_band + 1)), dma((2,)),
             dma((devices, 2)), dma((devices, sets)), dma((sets,)), dma((sets,)), dma,
             *(line * sets),
         ],
@@ -569,13 +660,17 @@
         in_specs=[
             smem,
             pl.BlockSpec((sets - 1, steps, devices * share, lanes), lambda i: (0, ahead + i, 0, 0)),
-            vmem,
+            hbm,
             table_block,
             hbm,
         ],
         out_specs=pl.BlockSpec((samples, steps, channels, longitudes), lambda i: (0, ahead + i, 0, 0)),
         out_shape=shape,
-        scratch_shapes=[pltpu.VMEM((devices * share, padded, lanes), jnp.float32)],
+        scratch_shapes=[
+            pltpu.VMEM((devices, share, padded, lanes), bf16),
+            pltpu.VMEM((devices * share, padded, lanes), jnp.float32),
+            dma,
+        ],
         input_output_aliases={4: 0},
         compiler_params=plain,
         cost_estimate=cost(block_rows),

time: 194 us -> 187 us (0.964)
  Pallas kernels: 186 us -> 181 us
  local copies, waits for them, and re-layouts: 3.88 us -> 1.05 us
    pallas_call x1, Pallas kernels: 155 us -> 149 us  [body(): pl.pallas_call(functools.partial(spectral_kernel, devices=devices, chips=...]
    pad x1 -> x0, local copies, waits for them, and re-layouts: 2.83 us -> none  [body(): legendre = jnp.pad(legendre, ((0, 0), (0, padded - block_rows), (0, 0)))]
where the time goes in v5:
time: 187 us; the launch traced here: 186 us
  Pallas kernels  181 us (97%)
  starting transfers between devices  3.54 us (2%)
    pallas_call x1, Pallas kernels, body(): pl.pallas_call(functools.partial(spectral_kernel, devices=devices, chips=...  149 us
    pallas_call x1, Pallas kernels, body(): pl.pallas_call(functools.partial(second_kernel, offset=early_lat), grid=(...  16.8 us
    pallas_call x1, Pallas kernels, body(): pl.pallas_call(first_kernel, grid=(ahead,), in_specs=[smem, pl.BlockSpec(...  15.3 us
  transfers between devices with their start and end apart: 1, of which 0 were waited for; matrix products, arithmetic and copies ran while one was open for 0% of the time, Pallas kernels for 8%

profile of v5, /device:TPU:0, one launch (start us, length us, event | category | flops | bytes accessed | tf_op | source)
XLA Modules:
  0.0 186.3 jit_solution(17273049701824269756)
XLA Ops:
  0.0 149.4 %spectral.1 = (bf16[2,180,16,384]{3,2,1,0:T(8,128)(2,1)}, bf16[90,16,384]{2,1,0:T(8,128)(2,1)}, bf16[4,4,96,384]{3,2,1,0:T(8,128)(2,1)}, bf16[192,1440]{1,0:T(8,...) custom-call(s32[48]{0:T(128)} %low_ref.1, ...), custom_call_target="tpu_custom_call" | custom-call | tf_op jit(solution)/shard_map/spectral/pallas_call | solution.py:585
  149.5 3.5 %all-to-all-start = ((bf16[4,4,96,384]{3,2,1,0:T(8,128)(2,1)}), bf16[4,4,96,384]{3,2,1,0:T(8,128)(2,1)S(1)}, u32[]{:S(2)}, u32[]{:S(2)}) async-start(bf16[4,4,96,384]{3,2,1,0:T(8,128)(2,1)} %get-tuple-element.10), calls=%async_computation | async-start | bytes 2359296 | tf_op jit(solution)/shard_map/all_to_all | solution.py:627
  153.0 15.3 %fourier_back.1._ = bf16[3,180,32,1440]{3,2,1,0:T(8,128)(2,1)} custom-call(f32[180]{0:T(256)} %weight_ref.3, bf16[2,180,16,384]{3,2,1,0:T(8,128)(2,1)} %get-tuple-element.9.band_ref, bf16[90,16,384]{2,1,0:T(8,128)(2,1)} %get-tuple-element.12.last_ref, bf16[192,1440]{1,0:T(8,128)(2,1)} %get-tuple-element.11.table_ref), custom_call_target="tpu_custom_call" | custom-call | flops 4777574400 | bytes 28200960 | tf_op jit(solution)/shard_map/fourier_back/pallas_call | solution.py:642
  168.3 0.0 all-to-all-done.source_ref
  168.3 0.0 copy-start
  168.3 1.0 copy-done
  169.3 16.8 %fourier_back_rest.1 = bf16[3,180,32,1440]{3,2,1,0:T(8,128)(2,1)} custom-call(f32[180]{0:T(256)} %weight_ref.3, bf16[2,180,16,384]{3,2,1,0:T(8,128)(2,1)} %get-tuple-element.9.band_ref, bf16[4,4,96,384]{3,2,1,0:T(8,128)(2,1)} %copy-done, bf16[192,1440]{1,0:T(8,128)(2,1)} %get-tuple-element.11.table_ref, ...), custom_call_target="tpu_custom_call", output_to_operand_aliasing={{}: (4, {})} | custom-call | flops 4777574400 | bytes 28200960 | tf_op jit(solution)/shard_map/fourier_back_rest/pallas_call | solution.py:657
Async XLA Ops:
  149.5 18.8 %all-to-all-start = ((bf16[4,4,96,384]{3,2,1,0:T(8,128)(2,1)}), bf16[4,4,96,384]{3,2,1,0:T(8,128)(2,1)S(1)}, u32[]{:S(2)}, u32[]{:S(2)}) async-start(bf16[4,4,96,384]{3,2,1,0:T(8,128)(2,1)} %get-tuple-element.10), calls=%async_computation | async-start | bytes 2359296 | tf_op jit(solution)/shard_map/all_to_all | solution.py:627
  168.3 1.0 copy-start
